TPU v7x, 32 devices: a whole 2x2x4 slice. The times are simulated.
32 devices in a mesh: seq: 16 (over z, y, core), tp: 2 (over x).
Axes of the slice: x: 2, y: 2, z: 4, core: 2. Of those that a mesh axis runs over, the one named last changes fastest.
Arguments:
- queries: bfloat16 [8192, 2048], P('seq', 'tp'), may hold values from -9 to 9
- keys: bfloat16 [8192, 2048], P('seq', 'tp'), may hold values from -9 to 9
- values: bfloat16 [8192, 2048], P('seq', 'tp'), may hold values from -6 to 6
- residual: bfloat16 [8192, 2048], P(('seq', 'tp')), may hold values from -36 to 36
- out_weight: bfloat16 [2048, 2048], P('tp'), may hold values from -0.125 to 0.125
- norm_gain: float32 [2048], replicated, may hold values from 0.25 to 1.75
- router: bfloat16 [2048, 8], replicated, may hold values from -0.25 to 0.25
- gate_weight: bfloat16 [2048, 5504], P('seq', 'tp'), may hold values from -0.125 to 0.125
- up_weight: bfloat16 [2048, 5504], P('seq', 'tp'), may hold values from -0.125 to 0.125
- down_weight: bfloat16 [5504, 2048], P('tp', 'seq'), may hold values from -0.078125 to 0.078125
- gate_shrink: bfloat16 [2048, 128], replicated, may hold values from -0.125 to 0.125
- up_shrink: bfloat16 [2048, 128], replicated, may hold values from -0.125 to 0.125
- gate_widen_maps: bfloat16 [128, 5504], P(None, 'tp'), may hold values from -0.75 to 0.75
- upward_widen_maps: bfloat16 [128, 5504], P(None, 'tp'), may hold values from -0.75 to 0.75
- down_shrink: bfloat16 [5504, 128], P('tp'), may hold values from -0.078125 to 0.078125
- down_expand: bfloat16 [128, 2048], replicated, may hold values from -1.5 to 1.5
- routing: int32 [8192, 2], P('seq'), may hold values from 0 to 7, all different within a row
- doc_lengths: int32 [4], replicated, may hold values from 1 to 4096, 8192 in all
Outputs:
- output: bfloat16 [8192, 2048], P(('seq', 'tp'))
Inputs may be any that keep to these rules, and one draw needn't show every extreme that they name: `routing`: each row names two different experts. `doc_lengths`: the lengths sum to 8192.
All inputs are finite; a program needn't handle non-finite values.
Results may differ from a plain program's by a relative error of at most 0.015.
Values may be sent and summed in bfloat16 or wider, within the bound.
A program may use at most 128 MiB of HBM per device.

v0:
```python
import math

import jax
import jax.numpy as jnp
from jax import lax
from jax.sharding import PartitionSpec as P

HEAD = 128
EXPERTS = 8
RANK = 16
WINDOW = 4096


adapter_scale_factor = 2.0
epsilon = 1e-05
masked_score = -1e30


def from_behind(value, axis, steps):
    count = lax.axis_size(axis)
    initial, last = (max(0, -steps), min(count, count - steps))
    return lax.ppermute(value, axis, [(source, source + steps) for source in range(initial, last)])


def document_of(positions, doc_ends):
    return jnp.sum((positions[:, None] >= doc_ends[None, :]).astype(jnp.int32), axis=1)


def on_device(
    queries,
    keys,
    values,
    residual,
    out_weight,
    norm_gain,
    router,
    gate_weight,
    up_weight,
    down_weight,
    gate_shrink,
    up_shrink,
    gate_widen_maps,
    upward_widen_maps,
    down_shrink,
    down_expand,
    routing,
    doc_lengths,
):
    tokens_here = queries.shape[0]
    total_width = queries.shape[1]
    heads_here = total_width // HEAD
    reach_blocks = WINDOW // tokens_here
    seq_index = lax.axis_index("seq")
    stacked = jnp.stack((keys, values))
    held_blocks = from_behind(stacked, "seq", 1)
    for section_index in range(reach_blocks.bit_length() - 1):
        earlier = from_behind(held_blocks, "seq", 1 << section_index)
        held_blocks = jnp.concatenate((earlier, held_blocks), axis=1)
    window = jnp.concatenate((held_blocks, stacked), axis=1)
    key_count = window.shape[1]
    doc_ends = jnp.cumsum(doc_lengths)
    query_positions = seq_index * tokens_here + jnp.arange(tokens_here, dtype=jnp.int32)
    key_positions = (seq_index - reach_blocks) * tokens_here + jnp.arange(
        key_count, dtype=jnp.int32
    )
    visible = key_positions[None, :] <= query_positions[:, None]
    visible = visible & (query_positions[:, None] - key_positions[None, :] < WINDOW)
    visible = visible & (key_positions[None, :] >= 0)
    visible = visible & (
        document_of(query_positions, doc_ends)[:, None]
        == document_of(key_positions, doc_ends)[None, :]
    )
    score_scale = 1.0 / math.sqrt(HEAD)
    query_heads = queries.reshape(tokens_here, heads_here, HEAD).transpose(1, 0, 2)
    key_heads = window[0].reshape(key_count, heads_here, HEAD).transpose(1, 0, 2)
    value_heads = window[1].reshape(key_count, heads_here, HEAD).transpose(1, 0, 2)

    def one_head(operands):
        query_one, key_one, value_one = operands
        scores = (
            jnp.einsum("qd,kd->qk", query_one, key_one, preferred_element_type=jnp.float32)
            * score_scale
        )
        scores = jnp.where(visible, scores, masked_score)
        largest = jnp.max(scores, axis=1, keepdims=True)
        exponent = jnp.exp(scores - largest)
        attn_weights = (exponent / jnp.sum(exponent, axis=1, keepdims=True)).astype(jnp.bfloat16)
        return jnp.dot(attn_weights, value_one, preferred_element_type=jnp.float32).astype(
            jnp.bfloat16
        )

    attended = lax.map(one_head, (query_heads, key_heads, value_heads))
    attended = attended.transpose(1, 0, 2).reshape(tokens_here, total_width)
    projected = lax.psum_scatter(
        jnp.dot(attended, out_weight, preferred_element_type=jnp.float32),
        "tp",
        scatter_dimension=0,
        tiled=True,
    )
    after_attention_state = residual.astype(jnp.float32) + projected
    mean_square = jnp.mean(after_attention_state * after_attention_state, axis=1, keepdims=True)
    normed_own = (after_attention_state * lax.rsqrt(mean_square + epsilon) * norm_gain).astype(
        jnp.bfloat16
    )
    normed = lax.all_gather(normed_own, "tp", axis=0, tiled=True)
    rank_gate = jnp.dot(normed, gate_shrink, preferred_element_type=jnp.float32).astype(
        jnp.bfloat16
    )
    rank_up = jnp.dot(normed, up_shrink, preferred_element_type=jnp.float32).astype(jnp.bfloat16)
    logits = jnp.dot(normed, router, preferred_element_type=jnp.float32)
    expert_ids = jnp.arange(EXPERTS, dtype=jnp.int32)
    first_logit = jnp.sum(jnp.where(routing[:, 0:1] == expert_ids[None, :], logits, 0.0), axis=1)
    second_logit = jnp.sum(jnp.where(routing[:, 1:2] == expert_ids[None, :], logits, 0.0), axis=1)
    weight_first = jax.nn.sigmoid(first_logit - second_logit)[:, None]
    weight_second = jax.nn.sigmoid(second_logit - first_logit)[:, None]
    frozen_gate_output = jnp.dot(
        normed,
        lax.all_gather(gate_weight, "seq", axis=0, tiled=True),
        preferred_element_type=jnp.float32,
    )
    frozen_up_output = jnp.dot(
        normed,
        lax.all_gather(up_weight, "seq", axis=0, tiled=True),
        preferred_element_type=jnp.float32,
    )
    column_expert = jnp.arange(EXPERTS * RANK, dtype=jnp.int32) // RANK
    hiddens = []
    pickers = []
    for slot_index in range(2):
        picker = column_expert[None, :] == routing[:, slot_index : slot_index + 1]
        pickers.append(picker)
        selected_gate_widen = jnp.where(picker, rank_gate, jnp.zeros_like(rank_gate))
        selected_upward_widen = jnp.where(picker, rank_up, jnp.zeros_like(rank_up))
        gate_complete_output = frozen_gate_output + adapter_scale_factor * jnp.dot(
            selected_gate_widen, gate_widen_maps, preferred_element_type=jnp.float32
        )
        upward_complete_output = frozen_up_output + adapter_scale_factor * jnp.dot(
            selected_upward_widen, upward_widen_maps, preferred_element_type=jnp.float32
        )
        hiddens.append(jax.nn.silu(gate_complete_output) * upward_complete_output)
    mixture = (weight_first * hiddens[0] + weight_second * hiddens[1]).astype(jnp.bfloat16)
    shrunk_first = jnp.dot(
        hiddens[0].astype(jnp.bfloat16), down_shrink, preferred_element_type=jnp.float32
    )
    shrunk_second = jnp.dot(
        hiddens[1].astype(jnp.bfloat16), down_shrink, preferred_element_type=jnp.float32
    )
    rank_down = weight_first * jnp.where(pickers[0], shrunk_first, 0.0) + weight_second * jnp.where(
        pickers[1], shrunk_second, 0.0
    )
    downward_adapter_term = jnp.dot(
        mixture,
        lax.all_gather(down_weight, "seq", axis=1, tiled=True),
        preferred_element_type=jnp.float32,
    )
    downward_token_rows, rank_rows = (
        lax.psum_scatter(
            downward_adapter_term.astype(jnp.bfloat16), "tp", scatter_dimension=0, tiled=True
        ).astype(jnp.float32),
        lax.psum_scatter(
            rank_down.astype(jnp.bfloat16), "tp", scatter_dimension=0, tiled=True
        ).astype(jnp.float32),
    )
    low_rank_product = jnp.dot(
        rank_rows.astype(jnp.bfloat16), down_expand, preferred_element_type=jnp.float32
    )
    return (
        after_attention_state + downward_token_rows + adapter_scale_factor * low_rank_product
    ).astype(jnp.bfloat16)


def solution(mesh):
    placed = (
        P("seq", "tp"),
        P("seq", "tp"),
        P("seq", "tp"),
        P(("seq", "tp"), None),
        P("tp", None),
        P(),
        P(),
        P("seq", "tp"),
        P("seq", "tp"),
        P("tp", "seq"),
        P(),
        P(),
        P(None, "tp"),
        P(None, "tp"),
        P("tp", None),
        P(),
        P("seq", None),
        P(),
    )
    return jax.shard_map(
        on_device, mesh=mesh, in_specs=placed, out_specs=P(("seq", "tp"), None), check_vma=False
    )
```

profile of v0, /device:TPU:0, one launch (start us, length us, event | category | flops | bytes accessed | tf_op | source)
XLA Modules:
  0.0 907.2 jit_solution(18371292692780234825)
XLA Ops:
  11.2 2.5 collective-permute-start
  13.7 3.6 collective-permute-done
  17.4 23.8 %collective-permute-start.1 = (bf16[2,512,1024]{1,2,0:T(8,128)(2,1)S(1)}, bf16[2,512,1024]{1,2,0:T(8,128)(2,1)S(1)}, u32[]{:S(2)}, u32[]{:S(2)}) collective-permute-start(bf16[2,512,1024]{1,2,0:T(8,128)(2,1)S(1)} %collective-permute-done), channel_id=1, source_target_pairs={{0,2},{2,4},{4,6},{6,8},{8,10},{10,12},{12,14},{14,16},{16,18},{18... | collective-permute-start | bytes 6291464 | tf_op jit(solution)/shard_map/ppermute | solution.py:22
  41.2 3.6 collective-permute-done.1
  45.5 26.3 %collective-permute-start.2 = (bf16[2,1024,1024]{1,2,0:T(8,128)(2,1)S(1)}, bf16[2,1024,1024]{1,2,0:T(8,128)(2,1)S(1)}, u32[]{:S(2)}, u32[]{:S(2)}) collective-permute-start(bf16[2,1024,1024]{1,2,0:T(8,128)(2,1)S(1)} %pad_maximum_fusion.1), channel_id=1, source_target_pairs={{0,4},{2,6},{4,8},{6,10},{8,12},{10,14},{12,16},{14,18},{16,20},{1... | collective-permute-start | bytes 12582920 | tf_op jit(solution)/shard_map/ppermute | solution.py:22
  71.9 89.8 %collective-permute-done.2 = bf16[2,1024,1024]{1,2,0:T(8,128)(2,1)S(1)} collective-permute-done((bf16[2,1024,1024]{1,2,0:T(8,128)(2,1)S(1)}, bf16[2,1024,1024]{1,2,0:T(8,128)(2,1)S(1)}, u32[]{:S(2)}, u32[]{:S(2)}) %collective-permute-start.2) | collective-permute-done | bytes 4194336 | tf_op jit(solution)/shard_map/ppermute | solution.py:22
  161.6 4.5 pad_maximum_fusion
  166.2 7.8 collective-permute-start.3
  176.7 172.0 %collective-permute-done.3 = bf16[2,2048,1024]{1,2,0:T(8,128)(2,1)} collective-permute-done((bf16[2,2048,1024]{1,2,0:T(8,128)(2,1)}, bf16[2,2048,1024]{1,2,0:T(8,128)(2,1)}, u32[]{:S(2)}, u32[]{:S(2)}) %collective-permute-start.3) | collective-permute-done | bytes 8388640 | tf_op jit(solution)/shard_map/ppermute | solution.py:22
  348.7 8.3 constant_dynamic-update-slice_fusion.5
  357.1 4.8 constant_dynamic-update-slice_fusion.4
  366.5 14.5 %fusion.66 = (bf16[1,4608,1024]{1,2,0:T(8,128)(2,1)}, bf16[1,4608,1024]{1,2,0:T(8,128)(2,1)}) fusion(bf16[2,4608,1024]{1,2,0:T(8,128)(2,1)} %constant_dynamic-update-slice_fusion.1), kind=kLoop, calls=%fused_computation.92 | loop fusion | bytes 37748736 | tf_op jit(solution)/shard_map/slice | solution.py:76
  380.9 81.6 %while.11 = (s32[]{:T(128)}, bf16[8,512,128]{1,2,0:T(8,128)(2,1)S(1)}, bf16[8,512,128]{1,2,0:T(8,128)(2,1)}, bf16[8,4608,128]{1,2,0:T(8,128)(2,1)}, bf16[8,4608,...) while((s32[]{:T(128)}, ...), condition=%wide.region_6.7_spmd.clone, body=%wide.region_3.6_spmd.clone.sunk | while | flops 1243413504 | bytes 31514736 | solution.py:92
  380.9 5.7 fusion.97
  388.1 2.9 fusion.99
  391.1 5.7 fusion.97
  398.2 2.9 fusion.99
  401.3 5.7 fusion.97
  408.4 2.9 fusion.99
  411.5 5.7 fusion.97
  418.6 2.9 fusion.99
  421.6 5.7 fusion.97
  428.8 2.9 fusion.99
  431.8 5.7 fusion.97
  439.0 2.9 fusion.99
  442.0 5.7 fusion.97
  449.1 2.9 fusion.99
  452.2 5.7 fusion.97
  459.3 2.9 fusion.99
  462.6 6.6 fusion.68
  469.3 56.5 %reduce-scatter.4.cloned.1.call-done = f32[256,2048]{1,0:T(8,128)} async-done(((f32[512,2048]{1,0:T(8,128)}), f32[256,2048]{1,0:T(8,128)}) %reduce-scatter.4.cloned.1.call-update) | async-done | bytes 2097168 | tf_op jit(solution)/shard_map/reduce_scatter | solution.py:94
  527.8 2.9 multiply_convert_fusion
  532.8 31.3 %all-gather.5.cloned.1.call-done = bf16[512,2048]{1,0:T(8,128)(2,1)} async-done(((bf16[256,2048]{1,0:T(8,128)(2,1)}), bf16[512,2048]{1,0:T(8,128)(2,1)}) %all-gather.5.cloned.1.call-update) | async-done | bytes 2097168 | tf_op jit(solution)/shard_map/all_gather | solution.py:105
  566.3 2.3 convolution_convert_fusion.2
  568.7 2.3 convolution_convert_fusion.1
  571.0 3.4 fusion.48
  574.4 3.4 fusion.47
  577.8 83.8 %all-gather.7.cloned.1.call-done = bf16[2048,2752]{0,1:T(8,128)(2,1)} async-done(((bf16[128,2752]{0,1:T(8,128)(2,1)}), bf16[2048,2752]{0,1:T(8,128)(2,1)}) %all-gather.7.cloned.1.call-update) | async-done | bytes 11272208 | tf_op jit(solution)/shard_map/all_gather | solution.py:118
  661.5 10.4 %fusion.69 = f32[512,2752]{0,1:T(8,128)} fusion(bf16[512,2048]{1,0:T(8,128)(2,1)S(1)} %copy-done.3, bf16[2048,2752]{0,1:T(8,128)(2,1)} %all-gather.7.cloned.1.call-done), kind=kOutput, calls=%fused_computation.95 | convolution fusion | flops 5771362304 | bytes 19005440 | tf_op jit(solution)/shard_map/dot_general | solution.py:116
  671.9 85.1 %all-gather.9.cloned.1.call-done = bf16[2048,2752]{0,1:T(8,128)(2,1)} async-done(((bf16[128,2752]{0,1:T(8,128)(2,1)}), bf16[2048,2752]{0,1:T(8,128)(2,1)}) %all-gather.9.cloned.1.call-update) | async-done | bytes 11272208 | tf_op jit(solution)/shard_map/all_gather | solution.py:123
  757.0 10.6 %fusion.70 = f32[512,2752]{0,1:T(8,128)} fusion(bf16[512,2048]{1,0:T(8,128)(2,1)S(1)} %copy-done.3, bf16[2048,2752]{0,1:T(8,128)(2,1)} %all-gather.9.cloned.1.call-done), kind=kOutput, calls=%fused_computation.96 | convolution fusion | flops 5771362304 | bytes 19005440 | tf_op jit(solution)/shard_map/dot_general | solution.py:121
  767.6 4.5 add_multiply_fusion.1
  773.1 3.6 copy-done.25
  778.9 2.4 copy-done.2
  783.1 69.4 %all-gather.11.cloned.1.call-done = bf16[2752,2048]{1,0:T(8,128)(2,1)} async-done(((bf16[2752,128]{1,0:T(8,128)(2,1)}), bf16[2752,2048]{1,0:T(8,128)(2,1)}) %all-gather.11.cloned.1.call-update) | async-done | bytes 11272208 | tf_op jit(solution)/shard_map/all_gather | solution.py:153
  852.5 13.2 %convolution_convert_fusion = bf16[512,2048]{1,0:T(8,128)(2,1)} fusion(bf16[2752,2048]{1,0:T(8,128)(2,1)} %all-gather.11.cloned.1.call-done, f32[512,2752]{0,1:T(8,128)} %copy-done.2, f32[512,2752]{0,1:T(8,128)} %copy-done.1, f32[512]{0:T(512)S(1)} %get-tuple-element.111, f32[512]{0:T(512)S(1)} %get-tuple-element.112), kind=kOutput, calls=%fused_computation.26 | convolution fusion | flops 5778046976 | bytes 24645632 | tf_op jit(solution)/shard_map/dot_general | solution.py:151
  865.8 31.5 %reduce-scatter.6.cloned.1.call-done = bf16[256,2048]{1,0:T(8,128)(2,1)} async-done(((bf16[512,2048]{1,0:T(8,128)(2,1)}), bf16[256,2048]{1,0:T(8,128)(2,1)}) %reduce-scatter.6.cloned.1.call-update) | async-done | bytes 1048592 | tf_op jit(solution)/shard_map/reduce_scatter | solution.py:157
  897.3 3.1 fusion.28
  (118 shorter events, 36.0 us)
Async XLA Ops:
  6.5 564.4 %copy-start = (bf16[128,2752]{0,1:T(8,128)(2,1)S(1)}, bf16[128,2752]{0,1:T(8,128)(2,1)}, u32[]{:S(2)}) copy-start(bf16[128,2752]{0,1:T(8,128)(2,1)} %param.32) | copy-start | bytes 2113540
  6.5 519.3 %reduce-scatter.4.cloned.1.call-start = ((), (), s32[]{:S(2)}) async-start(), calls=%async_computation.3 | async-start | bytes 6291456 | tf_op jit(solution)/shard_map/reduce_scatter | solution.py:94
  8.1 1.9 copy-start.9
  10.0 1.0 copy-start.11
  11.2 6.2 collective-permute-start
  17.4 27.5 %collective-permute-start.1 = (bf16[2,512,1024]{1,2,0:T(8,128)(2,1)S(1)}, bf16[2,512,1024]{1,2,0:T(8,128)(2,1)S(1)}, u32[]{:S(2)}, u32[]{:S(2)}) collective-permute-start(bf16[2,512,1024]{1,2,0:T(8,128)(2,1)S(1)} %collective-permute-done), channel_id=1, source_target_pairs={{0,2},{2,4},{4,6},{6,8},{8,10},{10,12},{12,14},{14,16},{16,18},{18... | collective-permute-start | bytes 6291464 | tf_op jit(solution)/shard_map/ppermute | solution.py:22
  44.8 121.3 %copy-start.5 = (bf16[2,512,1024]{1,2,0:T(8,128)(2,1)}, bf16[2,512,1024]{1,2,0:T(8,128)(2,1)S(1)}, u32[]{:S(2)}) copy-start(bf16[2,512,1024]{1,2,0:T(8,128)(2,1)S(1)} %collective-permute-done.1) | copy-start | bytes 6291460
  45.5 130.8 %copy-start.23 = (s32[4]{0:T(128)S(1)}, s32[4]{0:T(128)}, u32[]{:S(2)}) copy-start(s32[4]{0:T(128)} %param.37) | copy-start | bytes 52
  45.5 116.1 %collective-permute-start.2 = (bf16[2,1024,1024]{1,2,0:T(8,128)(2,1)S(1)}, bf16[2,1024,1024]{1,2,0:T(8,128)(2,1)S(1)}, u32[]{:S(2)}, u32[]{:S(2)}) collective-permute-start(bf16[2,1024,1024]{1,2,0:T(8,128)(2,1)S(1)} %pad_maximum_fusion.1), channel_id=1, source_target_pairs={{0,4},{2,6},{4,8},{6,10},{8,12},{10,14},{12,16},{14,18},{16,20},{1... | collective-permute-start | bytes 12582920 | tf_op jit(solution)/shard_map/ppermute | solution.py:22
  161.6 4.5 copy-start.7
  166.2 182.6 %collective-permute-start.3 = (bf16[2,2048,1024]{1,2,0:T(8,128)(2,1)}, bf16[2,2048,1024]{1,2,0:T(8,128)(2,1)}, u32[]{:S(2)}, u32[]{:S(2)}) collective-permute-start(bf16[2,2048,1024]{1,2,0:T(8,128)(2,1)} %pad_maximum_fusion), channel_id=1, source_target_pairs={{0,8},{2,10},{4,12},{6,14},{8,16},{10,18},{12,20},{14,22},{16,24},... | collective-permute-start | bytes 25165832 | tf_op jit(solution)/shard_map/ppermute | solution.py:22
  357.1 4.8 copy-start.6
  361.9 3.0 copy-start.10
  361.9 3.0 copy-start.12
  366.5 14.5 %copy-start.15 = (bf16[8,512,128]{1,2,0:T(8,128)(2,1)S(1)}, bf16[8,512,128]{1,2,0:T(8,128)(2,1)}, u32[]{:S(2)}) copy-start(bf16[8,512,128]{1,2,0:T(8,128)(2,1)} %custom-call.1) | copy-start | bytes 3145732
  462.6 63.3 %copy-start.8 = (bf16[256,2048]{1,0:T(8,128)(2,1)S(1)}, bf16[256,2048]{1,0:T(8,128)(2,1)}, u32[]{:S(2)}) copy-start(bf16[256,2048]{1,0:T(8,128)(2,1)} %param.23) | copy-start | bytes 3145732
  469.2 58.6 %copy-start.20 = (f32[2048]{0:T(1024)S(1)}, f32[2048]{0:T(1024)}, u32[]{:S(2)}) copy-start(f32[2048]{0:T(1024)} %param.25) | copy-start | bytes 24580
  469.2 63.5 %copy-start.21 = (s32[512,2]{0,1:T(2,128)S(1)}, s32[512,2]{0,1:T(2,128)}, u32[]{:S(2)}) copy-start(s32[512,2]{0,1:T(2,128)} %param.36) | copy-start | bytes 12292
  469.2 94.8 %copy-start.19 = (bf16[2048,8]{0,1:T(8,128)(2,1)S(1)}, bf16[2048,8]{0,1:T(8,128)(2,1)}, u32[]{:S(2)}) copy-start(bf16[2048,8]{0,1:T(8,128)(2,1)} %param.26) | copy-start | bytes 98308
  469.2 97.1 %copy-start.17 = (bf16[2048,128]{1,0:T(8,128)(2,1)S(1)}, bf16[2048,128]{1,0:T(8,128)(2,1)}, u32[]{:S(2)}) copy-start(bf16[2048,128]{1,0:T(8,128)(2,1)} %param.30) | copy-start | bytes 1572868
  469.2 94.8 %all-gather.5.cloned.1.call-start = ((), (), s32[]{:S(2)}) async-start(), calls=%async_computation.4 | async-start | bytes 3145728 | tf_op jit(solution)/shard_map/all_gather | solution.py:105
  527.8 40.8 %copy-start.18 = (bf16[2048,128]{1,0:T(8,128)(2,1)S(1)}, bf16[2048,128]{1,0:T(8,128)(2,1)}, u32[]{:S(2)}) copy-start(bf16[2048,128]{1,0:T(8,128)(2,1)} %param.31) | copy-start | bytes 1572868
  530.8 130.7 %all-gather.7.cloned.1.call-start = ((), (), s32[]{:S(2)}) async-start(), calls=%async_computation.5 | async-start | bytes 11976704 | tf_op jit(solution)/shard_map/all_gather | solution.py:118
  531.5 225.5 %all-gather.9.cloned.1.call-start = ((), (), s32[]{:S(2)}) async-start(), calls=%async_computation.6 | async-start | bytes 11976704 | tf_op jit(solution)/shard_map/all_gather | solution.py:123
  532.1 320.4 %all-gather.11.cloned.1.call-start = ((), (), s32[]{:S(2)}) async-start(), calls=%async_computation.7 | async-start | bytes 11976704 | tf_op jit(solution)/shard_map/all_gather | solution.py:153
  532.7 333.1 %reduce-scatter.8.cloned.1.call-start = ((), (), s32[]{:S(2)}) async-start(), calls=%async_computation.9 | async-start | bytes 196608 | tf_op jit(solution)/shard_map/reduce_scatter | solution.py:160
  571.0 90.6 %copy-start.3 = (bf16[512,2048]{1,0:T(8,128)(2,1)S(1)}, bf16[512,2048]{1,0:T(8,128)(2,1)}, u32[]{:S(2)}) copy-start(bf16[512,2048]{1,0:T(8,128)(2,1)} %all-gather.5.cloned.1.call-done) | copy-start | bytes 6291460
  757.0 10.6 %copy-start.13 = (f32[512,2752]{0,1:T(8,128)S(1)}, f32[512,2752]{0,1:T(8,128)}, u32[]{:S(2)}) copy-start(f32[512,2752]{0,1:T(8,128)} %fusion.47) | copy-start | bytes 16908292
  757.0 10.6 %copy-start.22 = (bf16[128,2752]{0,1:T(8,128)(2,1)S(1)}, bf16[128,2752]{0,1:T(8,128)(2,1)}, u32[]{:S(2)}) copy-start(bf16[128,2752]{0,1:T(8,128)(2,1)} %param.33) | copy-start | bytes 2113540
  757.0 10.6 %copy-start.24 = (f32[512,2752]{0,1:T(8,128)S(1)}, f32[512,2752]{0,1:T(8,128)}, u32[]{:S(2)}) copy-start(f32[512,2752]{0,1:T(8,128)} %fusion.69) | copy-start | bytes 16908292
  757.0 16.1 %slice-start = ((s8[5636096]{0:T(1024)(128)(4,1)}), s8[4194304]{0:T(1024)(128)(4,1)S(1)}, s32[]{:S(2)}) async-start(s8[5636096]{0:T(1024)(128)(4,1)} %bitcast.75), calls=%async_computation.10 | async-start | bytes 8388608
  767.6 4.5 copy-start.14
  767.6 5.5 slice-start.1
  772.1 6.8 copy-start.1
  772.1 4.6 copy-start.25
  778.9 2.5 copy-start.2
  783.0 114.3 %copy-start.4 = (f32[256,2048]{1,0:T(8,128)S(1)}, f32[256,2048]{1,0:T(8,128)}, u32[]{:S(2)}) copy-start(f32[256,2048]{1,0:T(8,128)} %reduce-scatter.4.cloned.1.call-done) | copy-start | bytes 6291460
  783.0 114.3 %copy-start.16 = (bf16[128,2048]{1,0:T(8,128)(2,1)S(1)}, bf16[128,2048]{1,0:T(8,128)(2,1)}, u32[]{:S(2)}) copy-start(bf16[128,2048]{1,0:T(8,128)(2,1)} %param.35) | copy-start | bytes 1572868
  783.0 114.3 %reduce-scatter.6.cloned.1.call-start = ((), (), s32[]{:S(2)}) async-start(), calls=%async_computation.8 | async-start | bytes 3145728 | tf_op jit(solution)/shard_map/reduce_scatter | solution.py:157
Sparse Core Ops, SparseCore 0:
  469.3 56.4 reduce-scatter.3
  530.9 33.0 all-gather.4
  566.2 95.2 all-gather.6
  663.5 93.4 all-gather.8
  759.0 93.4 all-gather.10
  854.5 8.5 reduce-scatter.7
  865.9 31.3 reduce-scatter.5
where the time goes:
time: 908 us; the launch traced here: 907 us
  waiting for transfers between devices  628 us (69%)
  matrix products  136 us (15%)
  starting transfers between devices  60.8 us (7%)
  local copies, waits for them, and re-layouts  44.6 us (5%)
  other arithmetic  23.5 us (3%)
  between operations  13.9 us (2%)
    ppermute x4, waiting for transfers between devices, from_behind(): lax.ppermute(value, axis, [(source, source + steps) for source in range(i...  269 us
    all_gather x1, waiting for transfers between devices, on_device(): lax.all_gather(up_weight, 'seq', axis=0, tiled=True)  85.1 us
    all_gather x1, waiting for transfers between devices, on_device(): lax.all_gather(gate_weight, 'seq', axis=0, tiled=True)  83.8 us
    all_gather x1, waiting for transfers between devices, on_device(): lax.all_gather(down_weight, 'seq', axis=1, tiled=True)  69.4 us
    ppermute x4, starting transfers between devices, from_behind(): lax.ppermute(value, axis, [(source, source + steps) for source in range(i...  60.5 us
    reduce_scatter x1, waiting for transfers between devices, on_device(): lax.psum_scatter(jnp.dot(attended, out_weight, preferred_element_type=jnp...  56.5 us
    dot_general x8, matrix products, one_head(): jnp.einsum('qd,kd->qk', query_one, key_one, preferred_element_type=jnp.fl...  45.9 us
    reduce_scatter x1, waiting for transfers between devices, on_device(): lax.psum_scatter(downward_adapter_term.astype(jnp.bfloat16), 'tp', scatte...  31.5 us
  transfers between devices with their start and end apart: 11, of which 10 were waited for; matrix products, arithmetic and copies ran while one was open for 7% of the time, Pallas kernels for 0%

commit v1 on v0

v1 whole, which is shorter than its diff:
```python
import functools
import math

import jax
import jax.numpy as jnp
from jax import lax
from jax.experimental import pallas as pl
from jax.experimental.pallas import tpu as pltpu
from jax.sharding import PartitionSpec as P

HEAD = 128
EXPERTS = 8
RANK = 16
WINDOW = 4096


adapter_scale_factor = 2.0
epsilon = 1e-05
masked_score = -1e30


MESH = pl.DeviceIdType.MESH
KEY_TILE = 512


def greet_all(n, me):
    barrier = pltpu.get_barrier_semaphore()

    def greet(i, carry):
        pl.semaphore_signal(
            barrier, inc=1, device_id={"seq": lax.rem(me + i, n)}, device_id_type=MESH
        )
        return carry

    lax.fori_loop(1, n, greet, 0)
    pl.semaphore_wait(barrier, n - 1)


def spread_kernel(n, group, q_ref, kv_ref, q_out, kv_out, kv_s, kv_r, q_s, q_r, f_s, f_r, own_s, own_r, loc):
    me = lax.axis_index("seq")
    chips = n // 2
    chip, core = me // 2, lax.rem(me, 2)
    sib = chip * 2 + (1 - core)
    tokens = q_ref.shape[0]
    part = tokens // group
    greet_all(n, me)

    def rows(j):
        return pl.ds(pl.multiple_of(j * tokens, tokens), tokens)

    def q_rows(j):
        return pl.ds(pl.multiple_of(j * part, part), part)

    def cols(d):
        return pl.ds(pl.multiple_of((d // group) * HEAD, HEAD), HEAD)

    def kv_copy(kind, source, d, send, recv):
        return pltpu.make_async_remote_copy(
            src_ref=kv_ref.at[kind, :, cols(d)],
            dst_ref=kv_out.at[kind, rows(source), :],
            send_sem=send,
            recv_sem=recv,
            device_id={"seq": d},
            device_id_type=MESH,
        )

    def q_copy(source, d, send, recv):
        return pltpu.make_async_remote_copy(
            src_ref=q_ref.at[q_rows(lax.rem(d, group)), cols(d)],
            dst_ref=q_out.at[q_rows(source), :],
            send_sem=send,
            recv_sem=recv,
            device_id={"seq": d},
            device_id_type=MESH,
        )

    def forward(kind, source, send, recv):
        return pltpu.make_async_remote_copy(
            src_ref=kv_out.at[kind, rows(source), :],
            dst_ref=kv_out.at[kind, rows(source), :],
            send_sem=send,
            recv_sem=recv,
            device_id={"seq": sib},
            device_id_type=MESH,
        )

    def send(c, carry):
        for b in range(2):
            d = lax.rem(chip + c, chips) * 2 + b
            kv_copy(b, me, d, kv_s.at[c, b], kv_r.at[c, core]).start()
            q_copy(me, d, q_s.at[c, b], q_r.at[c, core]).start()
        return carry

    lax.fori_loop(1, chips, send, 0)
    for kind in range(2):
        kv_copy(kind, me, sib, own_s.at[kind], own_r.at[kind]).start()
    q_copy(me, sib, own_s.at[2], own_r.at[2]).start()
    local = [
        pltpu.make_async_copy(kv_ref.at[kind, :, cols(me)], kv_out.at[kind, rows(me), :], loc.at[kind])
        for kind in range(2)
    ]
    local.append(
        pltpu.make_async_copy(
            q_ref.at[q_rows(lax.rem(me, group)), cols(me)], q_out.at[q_rows(me), :], loc.at[2]
        )
    )
    for copy in local:
        copy.start()

    def pass_on(c, carry):
        for b in range(2):
            source = lax.rem(chip - c + chips, chips) * 2 + b
            kv_copy(core, source, sib, kv_s.at[c, b], kv_r.at[c, b]).wait_recv()
            forward(core, source, f_s.at[c, b], f_r.at[c, b]).start()
        return carry

    lax.fori_loop(1, chips, pass_on, 0)

    def finish(c, carry):
        for b in range(2):
            d = lax.rem(chip + c, chips) * 2 + b
            source = lax.rem(chip - c + chips, chips) * 2 + b
            kv_copy(b, me, d, kv_s.at[c, b], kv_r.at[c, core]).wait_send()
            q_copy(me, d, q_s.at[c, b], q_r.at[c, core]).wait_send()
            q_copy(source, sib, q_s.at[c, b], q_r.at[c, b]).wait_recv()
            forward(core, source, f_s.at[c, b], f_r.at[c, b]).wait_send()
            forward(1 - core, source, f_s.at[c, b], f_r.at[c, b]).wait_recv()
        return carry

    lax.fori_loop(1, chips, finish, 0)
    for kind in range(2):
        kv_copy(kind, me, sib, own_s.at[kind], own_r.at[kind]).wait_send()
        kv_copy(kind, sib, sib, own_s.at[kind], own_r.at[kind]).wait_recv()
    q_copy(me, sib, own_s.at[2], own_r.at[2]).wait_send()
    q_copy(sib, sib, own_s.at[2], own_r.at[2]).wait_recv()
    for copy in local:
        copy.wait()


def spread(n, group, queries, stacked):
    tokens = queries.shape[0]
    chips = n // 2
    dma = pltpu.SemaphoreType.DMA
    return pl.pallas_call(
        functools.partial(spread_kernel, n, group),
        out_shape=(
            jax.ShapeDtypeStruct((n * tokens // group, HEAD), queries.dtype),
            jax.ShapeDtypeStruct((2, n * tokens, HEAD), queries.dtype),
        ),
        in_specs=[pl.BlockSpec(memory_space=pl.ANY)] * 2,
        out_specs=(pl.BlockSpec(memory_space=pl.ANY),) * 2,
        scratch_shapes=[dma((chips, 2))] * 6 + [dma((3,))] * 3,
        compiler_params=pltpu.CompilerParams(collective_id=0, has_side_effects=True),
        cost_estimate=pl.CostEstimate(flops=0, bytes_accessed=200_000_000, transcendentals=0),
        name="spread_heads",
    )(queries, stacked)


def gather_kernel(n, group, x_ref, out_ref, s_sem, r_sem, loc):
    me = lax.axis_index("seq")
    tokens = out_ref.shape[0]
    part = tokens // group
    greet_all(n, me)

    def place(source):
        return out_ref.at[
            pl.ds(pl.multiple_of(lax.rem(source, group) * part, part), part),
            pl.ds(pl.multiple_of((source // group) * HEAD, HEAD), HEAD),
        ]

    def piece(d):
        return x_ref.at[pl.ds(pl.multiple_of(d * part, part), part), :]

    def copy(i, source, d):
        return pltpu.make_async_remote_copy(
            src_ref=piece(d),
            dst_ref=place(source),
            send_sem=s_sem.at[i],
            recv_sem=r_sem.at[i],
            device_id={"seq": d},
            device_id_type=MESH,
        )

    def send(i, carry):
        copy(i, me, lax.rem(me + i, n)).start()
        return carry

    lax.fori_loop(1, n, send, 0)
    own = pltpu.make_async_copy(piece(me), place(me), loc)
    own.start()

    def finish(i, carry):
        d = lax.rem(me + i, n)
        copy(i, me, d).wait_send()
        copy(i, lax.rem(me - i + n, n), d).wait_recv()
        return carry

    lax.fori_loop(1, n, finish, 0)
    own.wait()


def regather(n, group, heads, tokens, attended):
    dma = pltpu.SemaphoreType.DMA
    return pl.pallas_call(
        functools.partial(gather_kernel, n, group),
        out_shape=jax.ShapeDtypeStruct((tokens, heads * HEAD), attended.dtype),
        in_specs=[pl.BlockSpec(memory_space=pl.ANY)],
        out_specs=pl.BlockSpec(memory_space=pl.ANY),
        scratch_shapes=[dma((n,)), dma((n,)), dma],
        compiler_params=pltpu.CompilerParams(collective_id=1, has_side_effects=True),
        cost_estimate=pl.CostEstimate(flops=0, bytes_accessed=60_000_000, transcendentals=0),
        name="regather_heads",
    )(attended)


def attend_kernel(tokens, part, docs, scalars, q_ref, k_ref, v_ref, o_ref):
    block = pl.program_id(0)
    first = block * tokens + scalars[docs] * part
    last = first + part - 1
    start = jnp.int32(0)
    q_pos = first + lax.broadcasted_iota(jnp.int32, (part, 1), 0)
    low = jnp.maximum(q_pos - (WINDOW - 1), 0)
    for j in range(docs):
        end = scalars[j]
        start = jnp.where(first >= end, end, start)
        low = jnp.maximum(low, jnp.where(q_pos >= end, end, 0))
    start = jnp.maximum(start, jnp.maximum(first - (WINDOW - 1), 0))
    q = q_ref[...]
    scale = 1.0 / math.sqrt(HEAD)

    def step(tile, carry):
        m, total, acc = carry
        base = pl.multiple_of(tile * KEY_TILE, KEY_TILE)
        k = k_ref[pl.ds(base, KEY_TILE), :]
        v = v_ref[pl.ds(base, KEY_TILE), :]
        scores = lax.dot_general(
            q, k, (((1,), (1,)), ((), ())), preferred_element_type=jnp.float32
        ) * scale
        k_pos = base + lax.broadcasted_iota(jnp.int32, (part, KEY_TILE), 1)
        scores = jnp.where((k_pos >= low) & (k_pos <= q_pos), scores, masked_score)
        new_m = jnp.maximum(m, jnp.max(scores, axis=1, keepdims=True))
        weights = jnp.exp(scores - new_m)
        shrink = jnp.exp(m - new_m)
        total = total * shrink + jnp.sum(weights, axis=1, keepdims=True)
        acc = acc * shrink + jnp.dot(
            weights.astype(jnp.bfloat16), v, preferred_element_type=jnp.float32
        )
        return new_m, total, acc

    _, total, acc = lax.fori_loop(
        start // KEY_TILE,
        last // KEY_TILE + 1,
        step,
        (
            jnp.full((part, 1), masked_score, jnp.float32),
            jnp.zeros((part, 1), jnp.float32),
            jnp.zeros((part, HEAD), jnp.float32),
        ),
    )
    o_ref[...] = (acc / total).astype(o_ref.dtype)


def attend(n, tokens, part, docs, scalars, q, kv):
    return pl.pallas_call(
        functools.partial(attend_kernel, tokens, part, docs),
        out_shape=jax.ShapeDtypeStruct(q.shape, q.dtype),
        grid_spec=pltpu.PrefetchScalarGridSpec(
            num_scalar_prefetch=1,
            grid=(n,),
            in_specs=[
                pl.BlockSpec((part, HEAD), lambda i, s: (i, 0)),
                pl.BlockSpec((None, n * tokens, HEAD), lambda i, s: (0, 0, 0)),
                pl.BlockSpec((None, n * tokens, HEAD), lambda i, s: (1, 0, 0)),
            ],
            out_specs=pl.BlockSpec((part, HEAD), lambda i, s: (i, 0)),
        ),
        compiler_params=pltpu.CompilerParams(vmem_limit_bytes=40 * 1024 * 1024),
        cost_estimate=pl.CostEstimate(
            flops=20_000_000_000, bytes_accessed=8_000_000, transcendentals=20_000_000
        ),
        name="attend_docs",
    )(scalars, q, kv, kv)


def sum_rows(partial, axis):
    count = lax.axis_size(axis)
    if count != 2:
        return lax.psum_scatter(
            partial.astype(jnp.bfloat16), axis, scatter_dimension=0, tiled=True
        ).astype(jnp.float32)
    half = partial.shape[0] // 2
    me = lax.axis_index(axis)
    away = lax.dynamic_slice_in_dim(partial, (1 - me) * half, half, 0)
    here = lax.dynamic_slice_in_dim(partial, me * half, half, 0)
    come = lax.ppermute(away.astype(jnp.bfloat16), axis, [(0, 1), (1, 0)])
    return here.astype(jnp.float32) + come.astype(jnp.float32)


def all_rows(own, axis):
    count = lax.axis_size(axis)
    if count != 2:
        return lax.all_gather(own, axis, axis=0, tiled=True)
    come = lax.ppermute(own, axis, [(0, 1), (1, 0)])
    first = lax.axis_index(axis) == 0
    return jnp.concatenate((jnp.where(first, own, come), jnp.where(first, come, own)), axis=0)


def on_device(
    queries,
    keys,
    values,
    residual,
    out_weight,
    norm_gain,
    router,
    gate_weight,
    up_weight,
    down_weight,
    gate_shrink,
    up_shrink,
    gate_widen_maps,
    upward_widen_maps,
    down_shrink,
    down_expand,
    routing,
    doc_lengths,
):
    tokens_here = queries.shape[0]
    total_width = queries.shape[1]
    heads_here = total_width // HEAD
    seq_count = lax.axis_size("seq")
    group = seq_count // heads_here
    part = tokens_here // group
    seq_index = lax.axis_index("seq")
    stacked = jnp.stack((keys, values))
    head_queries, head_kv = spread(seq_count, group, queries, stacked)
    doc_ends = jnp.cumsum(doc_lengths)
    scalars = jnp.concatenate((doc_ends, lax.rem(seq_index, group)[None])).astype(jnp.int32)
    attended = attend(
        seq_count, tokens_here, part, doc_lengths.shape[0], scalars, head_queries, head_kv
    )
    attended = regather(seq_count, group, heads_here, tokens_here, attended)
    projected = sum_rows(
        jnp.dot(attended, out_weight, preferred_element_type=jnp.float32), "tp"
    )
    after_attention_state = residual.astype(jnp.float32) + projected
    mean_square = jnp.mean(after_attention_state * after_attention_state, axis=1, keepdims=True)
    normed_own = (after_attention_state * lax.rsqrt(mean_square + epsilon) * norm_gain).astype(
        jnp.bfloat16
    )
    normed = all_rows(normed_own, "tp")
    rank_gate = jnp.dot(normed, gate_shrink, preferred_element_type=jnp.float32).astype(
        jnp.bfloat16
    )
    rank_up = jnp.dot(normed, up_shrink, preferred_element_type=jnp.float32).astype(jnp.bfloat16)
    logits = jnp.dot(normed, router, preferred_element_type=jnp.float32)
    expert_ids = jnp.arange(EXPERTS, dtype=jnp.int32)
    first_logit = jnp.sum(jnp.where(routing[:, 0:1] == expert_ids[None, :], logits, 0.0), axis=1)
    second_logit = jnp.sum(jnp.where(routing[:, 1:2] == expert_ids[None, :], logits, 0.0), axis=1)
    weight_first = jax.nn.sigmoid(first_logit - second_logit)[:, None]
    weight_second = jax.nn.sigmoid(second_logit - first_logit)[:, None]
    frozen_gate_output = jnp.dot(
        normed,
        lax.all_gather(gate_weight, "seq", axis=0, tiled=True),
        preferred_element_type=jnp.float32,
    )
    frozen_up_output = jnp.dot(
        normed,
        lax.all_gather(up_weight, "seq", axis=0, tiled=True),
        preferred_element_type=jnp.float32,
    )
    column_expert = jnp.arange(EXPERTS * RANK, dtype=jnp.int32) // RANK
    hiddens = []
    pickers = []
    for slot_index in range(2):
        picker = column_expert[None, :] == routing[:, slot_index : slot_index + 1]
        pickers.append(picker)
        selected_gate_widen = jnp.where(picker, rank_gate, jnp.zeros_like(rank_gate))
        selected_upward_widen = jnp.where(picker, rank_up, jnp.zeros_like(rank_up))
        gate_complete_output = frozen_gate_output + adapter_scale_factor * jnp.dot(
            selected_gate_widen, gate_widen_maps, preferred_element_type=jnp.float32
        )
        upward_complete_output = frozen_up_output + adapter_scale_factor * jnp.dot(
            selected_upward_widen, upward_widen_maps, preferred_element_type=jnp.float32
        )
        hiddens.append(jax.nn.silu(gate_complete_output) * upward_complete_output)
    mixture = (weight_first * hiddens[0] + weight_second * hiddens[1]).astype(jnp.bfloat16)
    shrunk_first = jnp.dot(
        hiddens[0].astype(jnp.bfloat16), down_shrink, preferred_element_type=jnp.float32
    )
    shrunk_second = jnp.dot(
        hiddens[1].astype(jnp.bfloat16), down_shrink, preferred_element_type=jnp.float32
    )
    rank_down = weight_first * jnp.where(pickers[0], shrunk_first, 0.0) + weight_second * jnp.where(
        pickers[1], shrunk_second, 0.0
    )
    downward_adapter_term = jnp.dot(
        mixture,
        lax.all_gather(down_weight, "seq", axis=1, tiled=True),
        preferred_element_type=jnp.float32,
    )
    downward_token_rows = sum_rows(downward_adapter_term, "tp")
    rank_rows = sum_rows(rank_down, "tp")
    low_rank_product = jnp.dot(
        rank_rows.astype(jnp.bfloat16), down_expand, preferred_element_type=jnp.float32
    )
    return (
        after_attention_state + downward_token_rows + adapter_scale_factor * low_rank_product
    ).astype(jnp.bfloat16)


def solution(mesh):
    placed = (
        P("seq", "tp"),
        P("seq", "tp"),
        P("seq", "tp"),
        P(("seq", "tp"), None),
        P("tp", None),
        P(),
        P(),
        P("seq", "tp"),
        P("seq", "tp"),
        P("tp", "seq"),
        P(),
        P(),
        P(None, "tp"),
        P(None, "tp"),
        P("tp", None),
        P(),
        P("seq", None),
        P(),
    )
    return jax.shard_map(
        on_device, mesh=mesh, in_specs=placed, out_specs=P(("seq", "tp"), None), check_vma=False
    )
```

time: 908 us -> 415 us (0.46)
  waiting for transfers between devices: 628 us -> 149 us
  Pallas kernels: 0 us -> 167 us
  matrix products: 136 us -> 60.9 us
  starting transfers between devices: 60.8 us -> 4.96 us
  local copies, waits for them, and re-layouts: 44.6 us -> 6.85 us
  other arithmetic: 23.5 us -> 9.86 us
    ppermute x4, waiting for transfers between devices: 269 us -> 66.6 us  [the longest x3 44.4 us: sum_rows(): come = lax.ppermute(away.astype(jnp.bfloat16), axis, [(0, 1), (1, 0)])]
    pallas_call x0 -> x3, Pallas kernels: none -> 167 us  [the longest x1 78.2 us: spread(): pl.pallas_call(functools.partial(spread_kernel, n, group), out_shape=(jax...]
    reduce_scatter x3 -> x0, waiting for transfers between devices: 88.1 us -> none  [the longest x1 56.5 us: on_device(): lax.psum_scatter(jnp.dot(attended, out_weight, preferred_element_type=jnp...]
    all_gather x1, waiting for transfers between devices: 83.8 us -> 0.01 us  [on_device(): lax.all_gather(gate_weight, 'seq', axis=0, tiled=True)]
    all_gather x1, waiting for transfers between devices: 85.1 us -> 4.47 us  [on_device(): lax.all_gather(up_weight, 'seq', axis=0, tiled=True)]
    dot_general x16 -> x0, matrix products: 68.8 us -> none  [the longest x8 45.9 us: one_head(): jnp.einsum('qd,kd->qk', query_one, key_one, preferred_element_type=jnp.fl...]
    ppermute x4, starting transfers between devices: 60.5 us -> 4.88 us  [the longest x3 3.98 us: sum_rows(): come = lax.ppermute(away.astype(jnp.bfloat16), axis, [(0, 1), (1, 0)])]
    all_gather x1 -> x0, waiting for transfers between devices: 31.3 us -> none  [on_device(): normed = lax.all_gather(normed_own, 'tp', axis=0, tiled=True)]
  transfers between devices with their start and end apart: 11 -> 7, of which waited for: 10 -> 5; matrix products, arithmetic and copies ran while one was open for 7% -> 14% of each run, Pallas kernels for 0% -> 40%
where the time goes in v1:
time: 415 us; the launch traced here: 411 us
  Pallas kernels  167 us (40%)
  waiting for transfers between devices  149 us (36%)
  matrix products  60.9 us (15%)
  between operations  13.4 us (3%)
  other arithmetic  9.86 us (2%)
  local copies, waits for them, and re-layouts  6.85 us (2%)
  starting transfers between devices  4.96 us (1%)
    pallas_call x1, Pallas kernels, spread(): pl.pallas_call(functools.partial(spread_kernel, n, group), out_shape=(jax...  78.2 us
    all_gather x1, waiting for transfers between devices, on_device(): lax.all_gather(down_weight, 'seq', axis=1, tiled=True)  75.7 us
    pallas_call x1, Pallas kernels, regather(): pl.pallas_call(functools.partial(gather_kernel, n, group), out_shape=jax....  57.5 us
    ppermute x3, waiting for transfers between devices, sum_rows(): come = lax.ppermute(away.astype(jnp.bfloat16), axis, [(0, 1), (1, 0)])  44.4 us
    pallas_call x1, Pallas kernels, attend(): pl.pallas_call(functools.partial(attend_kernel, tokens, part, docs), out_...  30.9 us
    ppermute x1, waiting for transfers between devices, all_rows(): come = lax.ppermute(own, axis, [(0, 1), (1, 0)])  22.2 us
    dot_general x1, matrix products, on_device(): jnp.dot(mixture, lax.all_gather(down_weight, 'seq', axis=1, tiled=True),...  12.8 us
    dot_general x1, matrix products, on_device(): jnp.dot(normed, lax.all_gather(gate_weight, 'seq', axis=0, tiled=True), p...  11 us
  transfers between devices with their start and end apart: 7, of which 5 were waited for; matrix products, arithmetic and copies ran while one was open for 14% of the time, Pallas kernels for 40%

profile of v1, /device:TPU:0, one launch (start us, length us, event | category | flops | bytes accessed | tf_op | source)
XLA Modules:
  0.0 411.4 jit_solution(17937661969356739887)
XLA Ops:
  6.5 0.7 all-gather.4.cloned.1.call-update
  7.3 0.0 all-gather.6.cloned.1.call-start
  7.3 0.7 all-gather.6.cloned.1.call-update
  8.0 0.0 all-gather.8.cloned.1.call-start
  8.1 0.7 all-gather.8.cloned.1.call-update
  8.7 0.8 reduce-window.9
  9.6 3.1 pad_maximum_fusion.kv_ref
  12.6 78.2 %spread_heads.1 = (bf16[4096,128]{1,0:T(8,128)(2,1)}, bf16[2,8192,128]{2,1,0:T(8,128)(2,1)}) custom-call(bf16[512,1024]{1,0:T(8,128)(2,1)} %q_ref.1, bf16[2,512,1024]{2,1,0:T(8,128)(2,1)} %pad_maximum_fusion.kv_ref), custom_call_target="tpu_custom_call" | custom-call | bytes 200000000 | tf_op jit(solution)/shard_map/spread_heads/pallas_call | solution.py:144
  90.8 0.1 pad_add_fusion.scalars
  90.9 2.2 copy-done.3
  93.1 1.2 copy-done.4
  94.3 30.9 %attend_docs.1.x_ref = bf16[4096,128]{1,0:T(8,128)(2,1)S(1)} custom-call(s32[5]{0:T(128)S(1)} %pad_add_fusion.scalars, bf16[4096,128]{1,0:T(8,128)(2,1)S(1)} %copy-done.4, bf16[2,8192,128]{2,1,0:T(8,128)(2,1)S(1)} %copy-done.3, bf16[2,8192,128]{2,1,0:T(8,128)(2,1)S(1)} %copy-done.3), custom_call_target="tpu_custom_call" | custom-call | flops 20000000000 | bytes 8000000 | tf_op jit(solution)/shard_map/attend_docs/pallas_call | solution.py:264
  125.3 0.0 copy-start.2
  125.3 1.0 copy-done.2
  126.2 57.5 %regather_heads.1 = bf16[512,1024]{1,0:T(8,128)(2,1)} custom-call(bf16[4096,128]{1,0:T(8,128)(2,1)} %copy-done.2), custom_call_target="tpu_custom_call" | custom-call | bytes 60000000 | tf_op jit(solution)/shard_map/regather_heads/pallas_call | solution.py:204
  183.7 4.9 %fusion.45 = f32[512,2048]{1,0:T(8,128)S(1)} fusion(bf16[512,1024]{1,0:T(8,128)(2,1)} %regather_heads.1, bf16[1024,2048]{1,0:T(8,128)(2,1)} %param.22), kind=kOutput, calls=%fused_computation.69 | convolution fusion | flops 2147483648 | bytes 9437184 | tf_op jit(solution)/shard_map/dot_general | solution.py:344
  188.6 2.1 copy-done.7
  190.7 0.1 dynamic-slice_convert_fusion.1
  190.8 1.0 collective-permute-start
  191.8 22.6 %collective-permute-done = bf16[256,2048]{1,0:T(8,128)(2,1)} collective-permute-done((bf16[256,2048]{1,0:T(8,128)(2,1)S(1)}, bf16[256,2048]{1,0:T(8,128)(2,1)}, u32[]{:S(2)}, u32[]{:S(2)}) %collective-permute-start) | collective-permute-done | bytes 1048608 | tf_op jit(solution)/shard_map/ppermute | solution.py:295
  214.4 2.8 multiply_reduce_fusion
  217.3 0.0 copy-start.16
  217.3 1.2 multiply_convert_fusion
  218.5 0.9 collective-permute-start.1
  219.4 22.2 %collective-permute-done.1 = bf16[256,2048]{1,0:T(8,128)(2,1)} collective-permute-done((bf16[256,2048]{1,0:T(8,128)(2,1)}, bf16[256,2048]{1,0:T(8,128)(2,1)}, u32[]{:S(2)}, u32[]{:S(2)}) %collective-permute-start.1) | collective-permute-done | bytes 1048608 | tf_op jit(solution)/shard_map/ppermute | solution.py:303
  241.6 1.8 broadcast_select_fusion.1
  243.5 0.0 copy-start.9
  243.5 0.7 select_reduce_fusion.1
  244.2 0.7 convolution_convert_fusion
  244.9 0.0 copy-done.15
  244.9 0.7 convolution_convert_fusion.1
  245.7 3.4 fusion.22
  249.1 3.4 fusion.23
  252.5 11.0 %fusion.42 = f32[512,2752]{0,1:T(8,128)} fusion(bf16[2048,2752]{0,1:T(8,128)(2,1)} %all-gather.4.cloned.1.call-done, bf16[256,2048]{1,0:T(8,128)(2,1)} %copy-done.9, bf16[256,2048]{1,0:T(8,128)(2,1)} %copy-done.8), kind=kOutput, calls=%fused_computation.66 | convolution fusion | flops 5775556608 | bytes 19005440 | tf_op jit(solution)/shard_map/dot_general | solution.py:362
  263.5 4.5 %all-gather.6.cloned.1.call-done = bf16[2048,2752]{0,1:T(8,128)(2,1)} async-done(((bf16[128,2752]{0,1:T(8,128)(2,1)}), bf16[2048,2752]{0,1:T(8,128)(2,1)}) %all-gather.6.cloned.1.call-update) | async-done | bytes 11272208 | tf_op jit(solution)/shard_map/all_gather | solution.py:369
  267.9 9.7 %fusion.41 = f32[512,2752]{0,1:T(8,128)S(1)} fusion(bf16[2048,2752]{0,1:T(8,128)(2,1)} %all-gather.6.cloned.1.call-done, bf16[256,2048]{1,0:T(8,128)(2,1)} %copy-done.9, bf16[256,2048]{1,0:T(8,128)(2,1)} %copy-done.8), kind=kOutput, calls=%fused_computation.65 | convolution fusion | flops 5775556608 | bytes 19005440 | tf_op jit(solution)/shard_map/dot_general | solution.py:367
  277.7 6.2 %add_multiply_fusion.1 = f32[512,2752]{0,1:T(8,128)} fusion(f32[512,2752]{0,1:T(8,128)S(1)} %fusion.41, f32[512,2752]{0,1:T(8,128)S(1)} %copy-done.17, f32[512,2752]{0,1:T(8,128)} %fusion.22, bf16[128,2752]{0,1:T(8,128)(2,1)S(1)} %copy-done.13, bf16[512,128]{1,0:T(8,128)(2,1)S(1)} %convolution_convert_fusion, s32[128]{0:T(128)S(1)} %and_select_fusion, ...), kind=kOutput, calls=%fused_computation.2 | convolution fusion | flops 373522432 | bytes 23382528 | tf_op jit(solution)/shard_map/dot_general | solution.py:383
  283.9 4.0 add_multiply_fusion
  287.9 75.7 %all-gather.8.cloned.1.call-done = bf16[2752,2048]{1,0:T(8,128)(2,1)} async-done(((bf16[2752,128]{1,0:T(8,128)(2,1)}), bf16[2752,2048]{1,0:T(8,128)(2,1)}) %all-gather.8.cloned.1.call-update) | async-done | bytes 11272208 | tf_op jit(solution)/shard_map/all_gather | solution.py:399
  363.6 12.8 %fusion = f32[512,2048]{1,0:T(8,128)S(1)} fusion(bf16[2752,2048]{1,0:T(8,128)(2,1)} %all-gather.8.cloned.1.call-done, f32[512,2752]{0,1:T(8,128)} %add_multiply_fusion, f32[512,2752]{0,1:T(8,128)} %add_multiply_fusion.1, f32[512]{0:T(512)S(1)} %get-tuple-element.16, f32[512]{0:T(512)S(1)} %get-tuple-element.15), kind=kOutput, calls=%fused_computation.3 | convolution fusion | flops 5776998400 | bytes 26742784 | tf_op jit(solution)/shard_map/dot_general | solution.py:397
  376.4 0.1 dynamic-slice_convert_fusion
  376.6 1.6 collective-permute-start.2
  378.2 1.0 fusion.10
  379.2 0.0 copy-start.1
  379.2 1.0 fusion.19
  380.2 1.5 collective-permute-start.3
  381.6 21.7 %collective-permute-done.3 = bf16[256,128]{1,0:T(8,128)(2,1)S(1)} collective-permute-done((bf16[256,128]{1,0:T(8,128)(2,1)S(1)}, bf16[256,128]{1,0:T(8,128)(2,1)S(1)}, u32[]{:S(2)}, u32[]{:S(2)}) %collective-permute-start.3) | collective-permute-done | bytes 65568 | tf_op jit(solution)/shard_map/ppermute | solution.py:295
  403.4 1.5 add_convert_fusion.2
  (45 shorter events, 0.1 us)
Async XLA Ops:
  6.5 239.1 %copy-start = (bf16[128,2752]{0,1:T(8,128)(2,1)S(1)}, bf16[128,2752]{0,1:T(8,128)(2,1)}, u32[]{:S(2)}) copy-start(bf16[128,2752]{0,1:T(8,128)(2,1)} %param.30) | copy-start | bytes 2113540
  6.5 245.9 %all-gather.4.cloned.1.call-start = ((), (), s32[]{:S(2)}) async-start(), calls=%async_computation | async-start | bytes 11976704 | tf_op jit(solution)/shard_map/all_gather | solution.py:364
  7.3 260.7 %all-gather.6.cloned.1.call-start = ((), (), s32[]{:S(2)}) async-start(), calls=%async_computation.1 | async-start | bytes 11976704 | tf_op jit(solution)/shard_map/all_gather | solution.py:369
  8.0 355.6 %all-gather.8.cloned.1.call-start = ((), (), s32[]{:S(2)}) async-start(), calls=%async_computation.2 | async-start | bytes 11976704 | tf_op jit(solution)/shard_map/all_gather | solution.py:399
  90.9 2.2 copy-start.3
  93.1 1.2 copy-start.4
  125.3 1.0 copy-start.2
  188.6 2.1 copy-start.7
  190.7 26.6 %copy-start.11 = (f32[2048]{0:T(1024)S(1)}, f32[2048]{0:T(1024)}, u32[]{:S(2)}) copy-start(f32[2048]{0:T(1024)} %param.23) | copy-start | bytes 24580
  190.8 23.6 %collective-permute-start = (bf16[256,2048]{1,0:T(8,128)(2,1)S(1)}, bf16[256,2048]{1,0:T(8,128)(2,1)}, u32[]{:S(2)}, u32[]{:S(2)}) collective-permute-start(bf16[256,2048]{1,0:T(8,128)(2,1)S(1)} %dynamic-slice_convert_fusion.1), channel_id=1, source_target_pairs={{0,1},{1,0},{2,3},{3,2},{4,5},{5,4},{6,7},{7,6},{8,9},{9,8},{10,11... | collective-permute-start | bytes 3145736 | tf_op jit(solution)/shard_map/ppermute | solution.py:295
  191.8 27.6 %copy-start.12 = (s32[512,2]{0,1:T(2,128)S(1)}, s32[512,2]{0,1:T(2,128)}, u32[]{:S(2)}) copy-start(s32[512,2]{0,1:T(2,128)} %param.34) | copy-start | bytes 12292
  217.3 26.2 %copy-start.16 = (bf16[2048,8]{0,1:T(8,128)(2,1)S(1)}, bf16[2048,8]{0,1:T(8,128)(2,1)}, u32[]{:S(2)}) copy-start(bf16[2048,8]{0,1:T(8,128)(2,1)} %param.24) | copy-start | bytes 98308
  218.5 23.1 %collective-permute-start.1 = (bf16[256,2048]{1,0:T(8,128)(2,1)}, bf16[256,2048]{1,0:T(8,128)(2,1)}, u32[]{:S(2)}, u32[]{:S(2)}) collective-permute-start(bf16[256,2048]{1,0:T(8,128)(2,1)} %multiply_convert_fusion), channel_id=1, source_target_pairs={{0,1},{1,0},{2,3},{3,2},{4,5},{5,4},{6,7},{7,6},{8,9},{9,8},{10,11... | collective-permute-start | bytes 3145736 | tf_op jit(solution)/shard_map/ppermute | solution.py:303
  219.4 24.8 %copy-start.14 = (bf16[2048,128]{1,0:T(8,128)(2,1)S(1)}, bf16[2048,128]{1,0:T(8,128)(2,1)}, u32[]{:S(2)}) copy-start(bf16[2048,128]{1,0:T(8,128)(2,1)} %param.29) | copy-start | bytes 1572868
  243.5 2.2 copy-start.8
  243.5 2.2 copy-start.9
  243.5 1.4 copy-start.15
  263.5 14.2 %copy-start.13 = (bf16[128,2752]{0,1:T(8,128)(2,1)S(1)}, bf16[128,2752]{0,1:T(8,128)(2,1)}, u32[]{:S(2)}) copy-start(bf16[128,2752]{0,1:T(8,128)(2,1)} %param.31) | copy-start | bytes 2113540
  267.9 9.7 %copy-start.17 = (f32[512,2752]{0,1:T(8,128)S(1)}, f32[512,2752]{0,1:T(8,128)}, u32[]{:S(2)}) copy-start(f32[512,2752]{0,1:T(8,128)} %fusion.42) | copy-start | bytes 16908292
  277.7 6.2 %copy-start.5 = (f32[512,2752]{0,1:T(8,128)S(1)}, f32[512,2752]{0,1:T(8,128)}, u32[]{:S(2)}) copy-start(f32[512,2752]{0,1:T(8,128)} %fusion.23) | copy-start | bytes 16908292
  363.6 14.6 %slice-start.2 = ((s8[5636096]{0:T(1024)(128)(4,1)}), s8[4194304]{0:T(1024)(128)(4,1)S(1)}, s32[]{:S(2)}) async-start(s8[5636096]{0:T(1024)(128)(4,1)} %bitcast.24), calls=%async_computation.5 | async-start | bytes 8388608
  363.6 14.6 %slice-start.3 = ((s8[5636096]{0:T(1024)(128)(4,1)}), s8[1441792]{0:T(1024)(128)(4,1)S(1)}, s32[]{:S(2)}) async-start(s8[5636096]{0:T(1024)(128)(4,1)} %bitcast.24), calls=%async_computation.6 | async-start | bytes 2883584
  363.6 14.6 %copy-start.6 = (bf16[2752,128]{1,0:T(8,128)(2,1)S(1)}, bf16[2752,128]{1,0:T(8,128)(2,1)}, u32[]{:S(2)}) copy-start(bf16[2752,128]{1,0:T(8,128)(2,1)} %param.32) | copy-start | bytes 2113540
  376.4 2.7 slice-start
  376.6 2.6 slice-start.1
  376.6 26.8 %collective-permute-start.2 = (bf16[256,2048]{1,0:T(8,128)(2,1)S(1)}, bf16[256,2048]{1,0:T(8,128)(2,1)S(1)}, u32[]{:S(2)}, u32[]{:S(2)}) collective-permute-start(bf16[256,2048]{1,0:T(8,128)(2,1)S(1)} %dynamic-slice_convert_fusion), channel_id=1, source_target_pairs={{0,1},{1,0},{2,3},{3,2},{4,5},{5,4},{6,7},{7,6},{8,9},{9,8},{10,11... | collective-permute-start | bytes 3145736 | tf_op jit(solution)/shard_map/ppermute | solution.py:295
  379.1 24.2 %copy-start.10 = (bf16[128,2048]{1,0:T(8,128)(2,1)S(1)}, bf16[128,2048]{1,0:T(8,128)(2,1)}, u32[]{:S(2)}) copy-start(bf16[128,2048]{1,0:T(8,128)(2,1)} %param.33) | copy-start | bytes 1572868
  379.2 25.7 %copy-start.1 = (bf16[128,2752]{0,1:T(8,128)(2,1)S(1)}, bf16[128,2752]{0,1:T(8,128)(2,1)}, u32[]{:S(2)}) copy-start(bf16[128,2752]{0,1:T(8,128)(2,1)} %param.30) | copy-start | bytes 2113540
  380.2 23.2 %collective-permute-start.3 = (bf16[256,128]{1,0:T(8,128)(2,1)S(1)}, bf16[256,128]{1,0:T(8,128)(2,1)S(1)}, u32[]{:S(2)}, u32[]{:S(2)}) collective-permute-start(bf16[256,128]{1,0:T(8,128)(2,1)S(1)} %dynamic-slice_convert_fusion.2), channel_id=1, source_target_pairs={{0,1},{1,0},{2,3},{3,2},{4,5},{5,4},{6,7},{7,6},{8,9},{9,8},{10,11... | collective-permute-start | bytes 196616 | tf_op jit(solution)/shard_map/ppermute | solution.py:295
Sparse Core Ops, SparseCore 0:
  9.5 154.0 all-gather.3
  165.7 102.1 all-gather.5
  270.1 93.4 all-gather.7

commit v2 on v1

--- a/solution.py
+++ b/solution.py
@@ -156,57 +156,119 @@
     )(queries, stacked)
 
 
-def gather_kernel(n, group, x_ref, out_ref, s_sem, r_sem, loc):
-    me = lax.axis_index("seq")
-    tokens = out_ref.shape[0]
-    part = tokens // group
-    greet_all(n, me)
-
-    def place(source):
+def gather_kernel(n, tn, group, heads, rotate, x_ref, out_ref, s_sem, r_sem, loc):
+    me, mt = lax.axis_index("seq"), lax.axis_index("tp")
+    kept = out_ref.shape[0]
+    part = kept * tn // group
+    per = kept // part
+    head, sub = me // group, lax.rem(me, group)
+    owner = sub // per
+    mine = owner == mt
+    sources = tn * heads * per
+
+    def source_of(i):
+        t, h, q = i // (heads * per), lax.rem(i // per, heads), lax.rem(i, per)
+        return h * group + mt * per + q, t
+
+    def place(h, q, t, u):
+        slot = lax.rem(t - u + tn, tn) if rotate else t
         return out_ref.at[
-            pl.ds(pl.multiple_of(lax.rem(source, group) * part, part), part),
-            pl.ds(pl.multiple_of((source // group) * HEAD, HEAD), HEAD),
+            pl.ds(pl.multiple_of(q * part, part), part),
+            pl.ds(pl.multiple_of((slot * heads + h) * HEAD, HEAD), HEAD),
         ]
 
     def piece(d):
         return x_ref.at[pl.ds(pl.multiple_of(d * part, part), part), :]
 
-    def copy(i, source, d):
+    barrier = pltpu.get_barrier_semaphore()
+
+    def greet(i, carry):
+        s, t = source_of(i)
+
+        @pl.when((s != me) | (t != mt))
+        def _():
+            pl.semaphore_signal(barrier, inc=1, device_id={"seq": s, "tp": t}, device_id_type=MESH)
+
+        return carry
+
+    lax.fori_loop(0, sources, greet, 0)
+    pl.semaphore_wait(barrier, n - jnp.where(mine, 1, 0))
+    own_id = (mt * heads + head) * per + lax.rem(sub, per)
+
+    def send_copy(d):
         return pltpu.make_async_remote_copy(
             src_ref=piece(d),
-            dst_ref=place(source),
-            send_sem=s_sem.at[i],
+            dst_ref=place(head, lax.rem(sub, per), mt, owner),
+            send_sem=s_sem.at[d],
+            recv_sem=r_sem.at[own_id],
+            device_id={"seq": d, "tp": owner},
+            device_id_type=MESH,
+        )
+
+    def receive(i):
+        t, h, q = i // (heads * per), lax.rem(i // per, heads), lax.rem(i, per)
+        return pltpu.make_async_remote_copy(
+            src_ref=piece(me),
+            dst_ref=place(h, q, t, mt),
+            send_sem=s_sem.at[me],
             recv_sem=r_sem.at[i],
-            device_id={"seq": d},
+            device_id={"seq": lax.rem(me + 1, n), "tp": owner},
             device_id_type=MESH,
         )
 
+    own = pltpu.make_async_copy(piece(me), place(head, lax.rem(sub, per), mt, mt), loc)
+
     def send(i, carry):
-        copy(i, me, lax.rem(me + i, n)).start()
+        send_copy(lax.rem(me + i, n)).start()
         return carry
 
     lax.fori_loop(1, n, send, 0)
-    own = pltpu.make_async_copy(piece(me), place(me), loc)
-    own.start()
-
-    def finish(i, carry):
-        d = lax.rem(me + i, n)
-        copy(i, me, d).wait_send()
-        copy(i, lax.rem(me - i + n, n), d).wait_recv()
-        return carry
-
-    lax.fori_loop(1, n, finish, 0)
-    own.wait()
-
-
-def regather(n, group, heads, tokens, attended):
+
+    @pl.when(mine)
+    def _():
+        own.start()
+
+    @pl.when(jnp.logical_not(mine))
+    def _():
+        send_copy(me).start()
+
+    def sent(i, carry):
+        send_copy(lax.rem(me + i, n)).wait_send()
+        return carry
+
+    lax.fori_loop(1, n, sent, 0)
+
+    def arrive(i, carry):
+        s, t = source_of(i)
+
+        @pl.when((s != me) | (t != mt))
+        def _():
+            receive(i).wait_recv()
+
+        return carry
+
+    lax.fori_loop(0, sources, arrive, 0)
+
+    @pl.when(mine)
+    def _():
+        own.wait()
+
+    @pl.when(jnp.logical_not(mine))
+    def _():
+        send_copy(me).wait_send()
+
+
+def regather(n, tn, group, heads, tokens, attended):
     dma = pltpu.SemaphoreType.DMA
+    kept = tokens // tn
+    part = tokens // group
+    assert kept % part == 0
     return pl.pallas_call(
-        functools.partial(gather_kernel, n, group),
-        out_shape=jax.ShapeDtypeStruct((tokens, heads * HEAD), attended.dtype),
+        functools.partial(gather_kernel, n, tn, group, heads, tn == 2),
+        out_shape=jax.ShapeDtypeStruct((kept, tn * heads * HEAD), attended.dtype),
         in_specs=[pl.BlockSpec(memory_space=pl.ANY)],
         out_specs=pl.BlockSpec(memory_space=pl.ANY),
-        scratch_shapes=[dma((n,)), dma((n,)), dma],
+        scratch_shapes=[dma((n,)), dma((tn * heads * (kept // part),)), dma],
         compiler_params=pltpu.CompilerParams(collective_id=1, has_side_effects=True),
         cost_estimate=pl.CostEstimate(flops=0, bytes_accessed=60_000_000, transcendentals=0),
         name="regather_heads",
@@ -282,28 +344,56 @@
     )(scalars, q, kv, kv)
 
 
-def sum_rows(partial, axis):
-    count = lax.axis_size(axis)
-    if count != 2:
-        return lax.psum_scatter(
-            partial.astype(jnp.bfloat16), axis, scatter_dimension=0, tiled=True
-        ).astype(jnp.float32)
-    half = partial.shape[0] // 2
-    me = lax.axis_index(axis)
-    away = lax.dynamic_slice_in_dim(partial, (1 - me) * half, half, 0)
-    here = lax.dynamic_slice_in_dim(partial, me * half, half, 0)
-    come = lax.ppermute(away.astype(jnp.bfloat16), axis, [(0, 1), (1, 0)])
-    return here.astype(jnp.float32) + come.astype(jnp.float32)
-
-
-def all_rows(own, axis):
-    count = lax.axis_size(axis)
-    if count != 2:
-        return lax.all_gather(own, axis, axis=0, tiled=True)
-    come = lax.ppermute(own, axis, [(0, 1), (1, 0)])
-    first = lax.axis_index(axis) == 0
-    return jnp.concatenate((jnp.where(first, own, come), jnp.where(first, come, own)), axis=0)
-
+def dot_t(rows, other):
+    return lax.dot_general(
+        rows, other, (((1,), (1,)), ((), ())), preferred_element_type=jnp.float32
+    )
+
+
+def feed_forward(normed, routing, weights, router, gate_shrink, up_shrink, gate_widen_maps, upward_widen_maps, down_shrink):
+    rank_gate = jnp.dot(normed, gate_shrink, preferred_element_type=jnp.float32).astype(
+        jnp.bfloat16
+    )
+    rank_up = jnp.dot(normed, up_shrink, preferred_element_type=jnp.float32).astype(jnp.bfloat16)
+    logits = jnp.dot(normed, router, preferred_element_type=jnp.float32)
+    expert_ids = jnp.arange(EXPERTS, dtype=jnp.int32)
+    first_logit = jnp.sum(jnp.where(routing[:, 0:1] == expert_ids[None, :], logits, 0.0), axis=1)
+    second_logit = jnp.sum(jnp.where(routing[:, 1:2] == expert_ids[None, :], logits, 0.0), axis=1)
+    weight_first = jax.nn.sigmoid(first_logit - second_logit)[:, None]
+    weight_second = jax.nn.sigmoid(second_logit - first_logit)[:, None]
+    frozen_gate_output = dot_t(normed, weights[0])
+    frozen_up_output = dot_t(normed, weights[1])
+    column_expert = jnp.arange(EXPERTS * RANK, dtype=jnp.int32) // RANK
+    hiddens = []
+    pickers = []
+    for slot_index in range(2):
+        picker = column_expert[None, :] == routing[:, slot_index : slot_index + 1]
+        pickers.append(picker)
+        selected_gate_widen = jnp.where(picker, rank_gate, jnp.zeros_like(rank_gate))
+        selected_upward_widen = jnp.where(picker, rank_up, jnp.zeros_like(rank_up))
+        gate_complete_output = frozen_gate_output + adapter_scale_factor * jnp.dot(
+            selected_gate_widen, gate_widen_maps, preferred_element_type=jnp.float32
+        )
+        upward_complete_output = frozen_up_output + adapter_scale_factor * jnp.dot(
+            selected_upward_widen, upward_widen_maps, preferred_element_type=jnp.float32
+        )
+        hiddens.append(jax.nn.silu(gate_complete_output) * upward_complete_output)
+    mixture = (weight_first * hiddens[0] + weight_second * hiddens[1]).astype(jnp.bfloat16)
+    shrunk_first = jnp.dot(
+        hiddens[0].astype(jnp.bfloat16), down_shrink, preferred_element_type=jnp.float32
+    )
+    shrunk_second = jnp.dot(
+        hiddens[1].astype(jnp.bfloat16), down_shrink, preferred_element_type=jnp.float32
+    )
+    rank_down = weight_first * jnp.where(pickers[0], shrunk_first, 0.0) + weight_second * jnp.where(
+        pickers[1], shrunk_second, 0.0
+    )
+    downward_adapter_term = jnp.dot(
+        mixture,
+        weights[2],
+        preferred_element_type=jnp.float32,
+    )
+    return downward_adapter_term.astype(jnp.bfloat16), rank_down.astype(jnp.bfloat16)
 
 def on_device(
     queries,
@@ -332,6 +422,10 @@
     group = seq_count // heads_here
     part = tokens_here // group
     seq_index = lax.axis_index("seq")
+    tp_count = lax.axis_size("tp")
+    weights = lax.all_gather(
+        jnp.stack((gate_weight.T, up_weight.T, down_weight)), "seq", axis=2, tiled=True
+    )
     stacked = jnp.stack((keys, values))
     head_queries, head_kv = spread(seq_count, group, queries, stacked)
     doc_ends = jnp.cumsum(doc_lengths)
@@ -339,68 +433,44 @@
     attended = attend(
         seq_count, tokens_here, part, doc_lengths.shape[0], scalars, head_queries, head_kv
     )
-    attended = regather(seq_count, group, heads_here, tokens_here, attended)
-    projected = sum_rows(
-        jnp.dot(attended, out_weight, preferred_element_type=jnp.float32), "tp"
-    )
+    attended = regather(seq_count, tp_count, group, heads_here, tokens_here, attended)
+    if tp_count == 2:
+        out_other = lax.ppermute(out_weight, "tp", [(0, 1), (1, 0)])
+        projected = jnp.dot(
+            attended[:, :total_width], out_weight, preferred_element_type=jnp.float32
+        ) + jnp.dot(attended[:, total_width:], out_other, preferred_element_type=jnp.float32)
+    else:
+        projected = jnp.dot(
+            attended,
+            lax.all_gather(out_weight, "tp", axis=0, tiled=True),
+            preferred_element_type=jnp.float32,
+        )
     after_attention_state = residual.astype(jnp.float32) + projected
     mean_square = jnp.mean(after_attention_state * after_attention_state, axis=1, keepdims=True)
     normed_own = (after_attention_state * lax.rsqrt(mean_square + epsilon) * norm_gain).astype(
         jnp.bfloat16
     )
-    normed = all_rows(normed_own, "tp")
-    rank_gate = jnp.dot(normed, gate_shrink, preferred_element_type=jnp.float32).astype(
-        jnp.bfloat16
-    )
-    rank_up = jnp.dot(normed, up_shrink, preferred_element_type=jnp.float32).astype(jnp.bfloat16)
-    logits = jnp.dot(normed, router, preferred_element_type=jnp.float32)
-    expert_ids = jnp.arange(EXPERTS, dtype=jnp.int32)
-    first_logit = jnp.sum(jnp.where(routing[:, 0:1] == expert_ids[None, :], logits, 0.0), axis=1)
-    second_logit = jnp.sum(jnp.where(routing[:, 1:2] == expert_ids[None, :], logits, 0.0), axis=1)
-    weight_first = jax.nn.sigmoid(first_logit - second_logit)[:, None]
-    weight_second = jax.nn.sigmoid(second_logit - first_logit)[:, None]
-    frozen_gate_output = jnp.dot(
-        normed,
-        lax.all_gather(gate_weight, "seq", axis=0, tiled=True),
-        preferred_element_type=jnp.float32,
-    )
-    frozen_up_output = jnp.dot(
-        normed,
-        lax.all_gather(up_weight, "seq", axis=0, tiled=True),
-        preferred_element_type=jnp.float32,
-    )
-    column_expert = jnp.arange(EXPERTS * RANK, dtype=jnp.int32) // RANK
-    hiddens = []
-    pickers = []
-    for slot_index in range(2):
-        picker = column_expert[None, :] == routing[:, slot_index : slot_index + 1]
-        pickers.append(picker)
-        selected_gate_widen = jnp.where(picker, rank_gate, jnp.zeros_like(rank_gate))
-        selected_upward_widen = jnp.where(picker, rank_up, jnp.zeros_like(rank_up))
-        gate_complete_output = frozen_gate_output + adapter_scale_factor * jnp.dot(
-            selected_gate_widen, gate_widen_maps, preferred_element_type=jnp.float32
-        )
-        upward_complete_output = frozen_up_output + adapter_scale_factor * jnp.dot(
-            selected_upward_widen, upward_widen_maps, preferred_element_type=jnp.float32
-        )
-        hiddens.append(jax.nn.silu(gate_complete_output) * upward_complete_output)
-    mixture = (weight_first * hiddens[0] + weight_second * hiddens[1]).astype(jnp.bfloat16)
-    shrunk_first = jnp.dot(
-        hiddens[0].astype(jnp.bfloat16), down_shrink, preferred_element_type=jnp.float32
-    )
-    shrunk_second = jnp.dot(
-        hiddens[1].astype(jnp.bfloat16), down_shrink, preferred_element_type=jnp.float32
-    )
-    rank_down = weight_first * jnp.where(pickers[0], shrunk_first, 0.0) + weight_second * jnp.where(
-        pickers[1], shrunk_second, 0.0
-    )
-    downward_adapter_term = jnp.dot(
-        mixture,
-        lax.all_gather(down_weight, "seq", axis=1, tiled=True),
-        preferred_element_type=jnp.float32,
-    )
-    downward_token_rows = sum_rows(downward_adapter_term, "tp")
-    rank_rows = sum_rows(rank_down, "tp")
+    shared = (router, gate_shrink, up_shrink, gate_widen_maps, upward_widen_maps, down_shrink)
+    if tp_count == 2:
+        swap = [(0, 1), (1, 0)]
+        half = tokens_here // 2
+        me = lax.axis_index("tp")
+        normed_away = lax.ppermute(normed_own, "tp", swap)
+        routing_own = lax.dynamic_slice_in_dim(routing, me * half, half, 0)
+        routing_away = lax.dynamic_slice_in_dim(routing, (1 - me) * half, half, 0)
+        away = feed_forward(normed_away, routing_away, weights, *shared)
+        come = [lax.ppermute(part_sum, "tp", swap) for part_sum in away]
+        normed_own, _ = lax.optimization_barrier((normed_own, away))
+        here = feed_forward(normed_own, routing_own, weights, *shared)
+        downward_token_rows, rank_rows = [
+            one.astype(jnp.float32) + two.astype(jnp.float32) for one, two in zip(here, come)
+        ]
+    else:
+        normed = lax.all_gather(normed_own, "tp", axis=0, tiled=True)
+        downward_token_rows, rank_rows = [
+            lax.psum_scatter(part_sum, "tp", scatter_dimension=0, tiled=True).astype(jnp.float32)
+            for part_sum in feed_forward(normed, routing, weights, *shared)
+        ]
     low_rank_product = jnp.dot(
         rank_rows.astype(jnp.bfloat16), down_expand, preferred_element_type=jnp.float32
     )

time: 415 us -> 343 us (0.83)
  waiting for transfers between devices: 149 us -> 66.6 us
  Pallas kernels: 167 us -> 179 us
  other arithmetic: 9.86 us -> 5.32 us
  matrix products: 60.9 us -> 65.2 us
    ppermute x4, waiting for transfers between devices: 66.6 us -> 24.1 us  [the longest x1 24.1 us: on_device(): normed_away = lax.ppermute(normed_own, 'tp', swap)]
    all_gather x3 -> x1, waiting for transfers between devices: 80.2 us -> 42.5 us  [on_device(): lax.all_gather(jnp.stack((gate_weight.T, up_weight.T, down_weight)), 'seq...]
    pallas_call x1, Pallas kernels: 30.9 us -> 37.9 us  [attend(): pl.pallas_call(functools.partial(attend_kernel, tokens, part, docs), out_...]
    dot_general x13 -> x25, matrix products: 59.4 us -> 59.9 us  [the longest x4 24.7 us: dot_t(): lax.dot_general(rows, other, (((1,), (1,)), ((), ())), preferred_element_...]
  transfers between devices with their start and end apart: 7 -> 5, of which waited for: 5 -> 2; matrix products, arithmetic and copies ran while one was open for 14% -> 11% of each run, Pallas kernels for 40% -> 52%
where the time goes in v2:
time: 343 us
  Pallas kernels  179 us (52%)
  waiting for transfers between devices  66.6 us (19%)
  matrix products  65.2 us (19%)
  between operations  13.8 us (4%)
  local copies, waits for them, and re-layouts  7.64 us (2%)
  starting transfers between devices  5.75 us (2%)
  other arithmetic  5.32 us (2%)
    pallas_call x1, Pallas kernels, spread(): pl.pallas_call(functools.partial(spread_kernel, n, group), out_shape=(jax...  79.6 us
    pallas_call x1, Pallas kernels, regather(): pl.pallas_call(functools.partial(gather_kernel, n, tn, group, heads, tn =...  61 us
    all_gather x1, waiting for transfers between devices, on_device(): lax.all_gather(jnp.stack((gate_weight.T, up_weight.T, down_weight)), 'seq...  42.5 us
    pallas_call x1, Pallas kernels, attend(): pl.pallas_call(functools.partial(attend_kernel, tokens, part, docs), out_...  37.9 us
    dot_general x4, matrix products, dot_t(): lax.dot_general(rows, other, (((1,), (1,)), ((), ())), preferred_element_...  24.7 us
    ppermute x1, waiting for transfers between devices, on_device(): normed_away = lax.ppermute(normed_own, 'tp', swap)  24.1 us
    dot_general x2, matrix products, feed_forward(): jnp.dot(mixture, weights[2], preferred_element_type=jnp.float32)  16.3 us
    unnamed x40, local copies, waits for them, and re-layouts  7.57 us
  transfers between devices with their start and end apart: 5, of which 2 were waited for; matrix products, arithmetic and copies ran while one was open for 11% of the time, Pallas kernels for 52%

profile of v2, /device:TPU:0, one launch (start us, length us, event | category | flops | bytes accessed | tf_op | source)
XLA Modules:
  0.0 342.9 jit_solution(15630118252761348912)
XLA Ops:
  6.6 3.3 pad_maximum_fusion
  9.9 3.0 collective-permute-start
  12.9 0.2 reduce-window.9
  13.1 1.5 pad_maximum_fusion.1.kv_ref
  14.6 79.6 %spread_heads.1 = (bf16[4096,128]{1,0:T(8,128)(2,1)}, bf16[2,8192,128]{2,1,0:T(8,128)(2,1)}) custom-call(bf16[512,1024]{1,0:T(8,128)(2,1)} %q_ref.1, bf16[2,512,1024]{2,1,0:T(8,128)(2,1)} %pad_maximum_fusion.1.kv_ref), custom_call_target="tpu_custom_call" | custom-call | bytes 200000000 | tf_op jit(solution)/shard_map/spread_heads/pallas_call | solution.py:144
  94.2 0.1 pad_add_fusion.scalars
  94.3 3.0 copy-done.2
  97.3 1.2 copy-done.3
  98.5 37.9 %attend_docs.1.x_ref = bf16[4096,128]{1,0:T(8,128)(2,1)S(1)} custom-call(s32[5]{0:T(128)S(1)} %pad_add_fusion.scalars, bf16[4096,128]{1,0:T(8,128)(2,1)S(1)} %copy-done.3, bf16[2,8192,128]{2,1,0:T(8,128)(2,1)S(1)} %copy-done.2, bf16[2,8192,128]{2,1,0:T(8,128)(2,1)S(1)} %copy-done.2), custom_call_target="tpu_custom_call" | custom-call | flops 20000000000 | bytes 8000000 | tf_op jit(solution)/shard_map/attend_docs/pallas_call | solution.py:326
  136.4 1.0 copy-done.1
  137.4 61.0 %regather_heads.1 = bf16[256,2048]{1,0:T(8,128)(2,1)} custom-call(bf16[4096,128]{1,0:T(8,128)(2,1)} %copy-done.1), custom_call_target="tpu_custom_call" | custom-call | bytes 60000000 | tf_op jit(solution)/shard_map/regather_heads/pallas_call | solution.py:266
  198.4 4.3 %fusion.74 = f32[256,2048]{1,0:T(8,128)S(1)} fusion(bf16[1024,2048]{1,0:T(8,128)(2,1)} %param.22, bf16[256,2048]{1,0:T(8,128)(2,1)} %regather_heads.1), kind=kOutput, calls=%fused_computation.72 | convolution fusion | flops 1073741824 | bytes 6815744 | tf_op jit(solution)/shard_map/dot_general | solution.py:439
  202.8 3.8 %multiply_reduce_fusion = (f32[256]{0:T(256)S(1)}, f32[256,2048]{1,0:T(8,128)S(1)}) fusion(f32[256,2048]{1,0:T(8,128)S(1)} %fusion.74, bf16[1024,2048]{1,0:T(8,128)(2,1)} %collective-permute-done, bf16[256,2048]{1,0:T(8,128)(2,1)S(1)} %copy-done.10, bf16[256,2048]{1,0:T(8,128)(2,1)S(1)} %copy-done.17), kind=kOutput, calls=%fused_computation.41 | convolution fusion | flops 1076363008 | bytes 9962496 | tf_op jit(solution)/shard_map/dot_general | solution.py:441
  206.7 1.3 copy-done.5
  208.0 0.2 multiply_convert_fusion
  208.2 0.6 collective-permute-start.1
  208.9 0.1 constant_dynamic-slice_fusion
  208.9 24.1 %collective-permute-done.1 = bf16[256,2048]{1,0:T(8,128)(2,1)S(1)} collective-permute-done((bf16[256,2048]{1,0:T(8,128)(2,1)S(1)}, bf16[256,2048]{1,0:T(8,128)(2,1)S(1)}, u32[]{:S(2)}, u32[]{:S(2)}) %collective-permute-start.1) | collective-permute-done | bytes 1048608 | tf_op jit(solution)/shard_map/ppermute | solution.py:458
  233.0 0.4 select_reduce_fusion.3
  233.5 0.4 convolution_convert_fusion.2
  233.9 0.4 convolution_convert_fusion.3
  234.3 42.5 %all-gather.2.cloned.1.call-done = bf16[3,2752,2048]{2,1,0:T(8,128)(2,1)} async-done(((bf16[3,2752,128]{2,1,0:T(8,128)(2,1)}), bf16[3,2752,2048]{2,1,0:T(8,128)(2,1)}) %all-gather.2.cloned.1.call-update) | async-done | bytes 33816592 | tf_op jit(solution)/shard_map/all_gather | solution.py:426
  276.9 6.0 %fusion.1 = f32[256,2752]{0,1:T(8,128)S(1)} fusion(bf16[256,2048]{1,0:T(8,128)(2,1)S(1)} %collective-permute-done.1, bf16[3,2752,2048]{2,1,0:T(8,128)(2,1)} %all-gather.2.cloned.1.call-done), kind=kOutput, calls=%fused_computation.4 | convolution fusion | flops 2885681152 | bytes 15138816 | tf_op jit(solution)/shard_map/dot_general | solution.py:348
  282.9 0.6 fusion.9
  283.5 0.6 fusion.6
  284.2 6.3 %fusion.3 = f32[256,2752]{0,1:T(8,128)S(1)} fusion(bf16[256,2048]{1,0:T(8,128)(2,1)S(1)} %collective-permute-done.1, bf16[3,2752,2048]{2,1,0:T(8,128)(2,1)} %all-gather.2.cloned.1.call-done), kind=kOutput, calls=%fused_computation.6 | convolution fusion | flops 2885681152 | bytes 15138816 | tf_op jit(solution)/shard_map/dot_general | solution.py:348
  290.5 1.0 fusion.8
  291.5 1.0 fusion.11
  292.6 0.1 copy-done.4
  292.6 0.6 fusion.46
  293.2 0.6 fusion.70
  293.8 7.6 %fusion.19 = bf16[256,2048]{1,0:T(8,128)(2,1)S(1)} fusion(bf16[3,2752,2048]{2,1,0:T(8,128)(2,1)} %all-gather.2.cloned.1.call-done, f32[256,2752]{0,1:T(8,128)S(1)} %fusion.11, f32[256,2752]{0,1:T(8,128)S(1)} %fusion.8, f32[256]{0:T(256)S(1)} %get-tuple-element.22, f32[256]{0:T(256)S(1)} %get-tuple-element.21), kind=kOutput, calls=%fused_computation.34 | convolution fusion | flops 2889023488 | bytes 17958912 | tf_op jit(solution)/shard_map/dot_general | solution.py:391
  301.5 0.4 convolution_convert_fusion
  301.9 0.4 convolution_convert_fusion.1
  302.3 0.1 collective-permute-start.3
  302.4 2.0 collective-permute-start.2
  304.4 0.4 select_reduce_fusion.1
  304.8 6.1 %fusion = f32[256,2752]{0,1:T(8,128)S(1)} fusion(bf16[256,2048]{1,0:T(8,128)(2,1)S(1)} %multiply_convert_fusion, bf16[3,2752,2048]{2,1,0:T(8,128)(2,1)} %all-gather.2.cloned.1.call-done), kind=kOutput, calls=%fused_computation.3 | convolution fusion | flops 2885681152 | bytes 15138816 | tf_op jit(solution)/shard_map/dot_general | solution.py:348
  310.9 0.6 fusion.15
  311.5 0.6 fusion.12
  312.1 6.3 %fusion.2 = f32[256,2752]{0,1:T(8,128)S(1)} fusion(bf16[256,2048]{1,0:T(8,128)(2,1)S(1)} %multiply_convert_fusion, bf16[3,2752,2048]{2,1,0:T(8,128)(2,1)} %all-gather.2.cloned.1.call-done), kind=kOutput, calls=%fused_computation.5 | convolution fusion | flops 2885681152 | bytes 15138816 | tf_op jit(solution)/shard_map/dot_general | solution.py:348
  318.4 1.0 fusion.14
  319.5 1.0 fusion.17
  320.5 0.5 copy-done.6
  321.0 8.7 %fusion.21 = f32[256,2048]{1,0:T(8,128)} fusion(bf16[3,2752,2048]{2,1,0:T(8,128)(2,1)} %all-gather.2.cloned.1.call-done, f32[256,2752]{0,1:T(8,128)S(1)} %fusion.17, f32[256,2752]{0,1:T(8,128)S(1)} %fusion.14, f32[256]{0:T(256)S(1)} %get-tuple-element.20, f32[256]{0:T(256)S(1)} %get-tuple-element.19), kind=kOutput, calls=%fused_computation.36 | convolution fusion | flops 2889547776 | bytes 19007488 | tf_op jit(solution)/shard_map/dot_general | solution.py:391
  329.7 0.6 fusion.61
  330.3 0.4 copy-done.13
  330.7 5.3 %add_convert_fusion.2 = bf16[256,2048]{1,0:T(8,128)(2,1)} fusion(f32[256,2048]{1,0:T(8,128)} %copy-done.5, f32[256,2048]{1,0:T(8,128)} %fusion.21, bf16[256,2048]{1,0:T(8,128)(2,1)} %collective-permute-done.2, bf16[128,2048]{1,0:T(8,128)(2,1)S(1)} %copy-done.13, bf16[256,128]{1,0:T(8,128)(2,1)S(1)} %collective-permute-done.3, f32[256,128]{1,0:T(8,128)S(1)} %fusion.61, ...), kind=kOutput, calls=%fused_computation.39 | convolution fusion | flops 318717952 | bytes 10537472 | tf_op jit(solution)/shard_map/dot_general | solution.py:474
  (42 shorter events, 0.1 us)
Async XLA Ops:
  6.5 276.4 %copy-start = (bf16[128,2752]{0,1:T(8,128)(2,1)S(1)}, bf16[128,2752]{0,1:T(8,128)(2,1)}, u32[]{:S(2)}) copy-start(bf16[128,2752]{0,1:T(8,128)(2,1)} %param.30) | copy-start | bytes 2113540
  6.5 270.3 %all-gather.2.cloned.1.call-start = ((), (), s32[]{:S(2)}) async-start(), calls=%async_computation | async-start | bytes 35930112 | tf_op jit(solution)/shard_map/all_gather | solution.py:426
  6.5 6.4 %copy-start.19 = (s32[4]{0:T(128)S(1)}, s32[4]{0:T(128)}, u32[]{:S(2)}) copy-start(s32[4]{0:T(128)} %param.35) | copy-start | bytes 52
  6.5 6.5 %copy-start.11 = (bf16[512,1024]{1,0:T(8,128)(2,1)S(1)}, bf16[512,1024]{1,0:T(8,128)(2,1)}, u32[]{:S(2)}) copy-start(bf16[512,1024]{1,0:T(8,128)(2,1)} %param.20) | copy-start | bytes 3145732
  6.5 6.5 %copy-start.12 = (bf16[512,1024]{1,0:T(8,128)(2,1)S(1)}, bf16[512,1024]{1,0:T(8,128)(2,1)}, u32[]{:S(2)}) copy-start(bf16[512,1024]{1,0:T(8,128)(2,1)} %param.19) | copy-start | bytes 3145732
  9.9 192.9 %collective-permute-start = (bf16[1024,2048]{1,0:T(8,128)(2,1)}, bf16[1024,2048]{1,0:T(8,128)(2,1)}, u32[]{:S(2)}, u32[]{:S(2)}) collective-permute-start(bf16[1024,2048]{1,0:T(8,128)(2,1)} %param.22), channel_id=1, source_target_pairs={{0,1},{1,0},{2,3},{3,2},{4,5},{5,4},{6,7},{7,6},{8,9},{9,8},{10,11... | collective-permute-start | bytes 12582920 | tf_op jit(solution)/shard_map/ppermute | solution.py:438
  94.3 3.0 copy-start.2
  97.3 1.2 copy-start.3
  136.4 1.0 copy-start.1
  198.4 4.4 %copy-start.10 = (bf16[256,2048]{1,0:T(8,128)(2,1)S(1)}, bf16[256,2048]{1,0:T(8,128)(2,1)}, u32[]{:S(2)}) copy-start(bf16[256,2048]{1,0:T(8,128)(2,1)} %regather_heads.1) | copy-start | bytes 3145732
  198.4 4.4 %copy-start.17 = (bf16[256,2048]{1,0:T(8,128)(2,1)S(1)}, bf16[256,2048]{1,0:T(8,128)(2,1)}, u32[]{:S(2)}) copy-start(bf16[256,2048]{1,0:T(8,128)(2,1)} %param.21) | copy-start | bytes 3145732
  202.8 5.2 %copy-start.15 = (f32[2048]{0:T(1024)S(1)}, f32[2048]{0:T(1024)}, u32[]{:S(2)}) copy-start(f32[2048]{0:T(1024)} %param.23) | copy-start | bytes 24580
  206.6 1.4 copy-start.5
  206.6 2.2 copy-start.16
  206.6 26.4 %copy-start.14 = (bf16[2048,8]{0,1:T(8,128)(2,1)S(1)}, bf16[2048,8]{0,1:T(8,128)(2,1)}, u32[]{:S(2)}) copy-start(bf16[2048,8]{0,1:T(8,128)(2,1)} %param.24) | copy-start | bytes 98308
  206.6 26.8 %copy-start.7 = (bf16[2048,128]{1,0:T(8,128)(2,1)S(1)}, bf16[2048,128]{1,0:T(8,128)(2,1)}, u32[]{:S(2)}) copy-start(bf16[2048,128]{1,0:T(8,128)(2,1)} %param.29) | copy-start | bytes 1572868
  208.2 24.8 %collective-permute-start.1 = (bf16[256,2048]{1,0:T(8,128)(2,1)S(1)}, bf16[256,2048]{1,0:T(8,128)(2,1)S(1)}, u32[]{:S(2)}, u32[]{:S(2)}) collective-permute-start(bf16[256,2048]{1,0:T(8,128)(2,1)S(1)} %multiply_convert_fusion), channel_id=1, source_target_pairs={{0,1},{1,0},{2,3},{3,2},{4,5},{5,4},{6,7},{7,6},{8,9},{9,8},{10,11... | collective-permute-start | bytes 3145736 | tf_op jit(solution)/shard_map/ppermute | solution.py:458
  208.9 25.0 %copy-start.8 = (bf16[2048,128]{1,0:T(8,128)(2,1)S(1)}, bf16[2048,128]{1,0:T(8,128)(2,1)}, u32[]{:S(2)}) copy-start(bf16[2048,128]{1,0:T(8,128)(2,1)} %param.28) | copy-start | bytes 1572868
  284.1 6.3 %copy-start.18 = (bf16[128,2752]{0,1:T(8,128)(2,1)S(1)}, bf16[128,2752]{0,1:T(8,128)(2,1)}, u32[]{:S(2)}) copy-start(bf16[128,2752]{0,1:T(8,128)(2,1)} %param.31) | copy-start | bytes 2113540
  291.5 1.1 copy-start.4
  293.8 8.1 %copy-start.9 = (bf16[2048,128]{1,0:T(8,128)(2,1)S(1)}, bf16[2048,128]{1,0:T(8,128)(2,1)}, u32[]{:S(2)}) copy-start(bf16[2048,128]{1,0:T(8,128)(2,1)} %param.28) | copy-start | bytes 1572868
  302.3 27.9 %collective-permute-start.3 = (bf16[256,128]{1,0:T(8,128)(2,1)S(1)}, bf16[256,128]{1,0:T(8,128)(2,1)S(1)}, u32[]{:S(2)}, u32[]{:S(2)}) collective-permute-start(bf16[256,128]{1,0:T(8,128)(2,1)S(1)} %fusion.70), channel_id=1, source_target_pairs={{0,1},{1,0},{2,3},{3,2},{4,5},{5,4},{6,7},{7,6},{8,9},{9,8},{10,11... | collective-permute-start | bytes 196616 | tf_op jit(solution)/shard_map/ppermute | solution.py:462
  302.4 27.9 %collective-permute-start.2 = (bf16[256,2048]{1,0:T(8,128)(2,1)S(1)}, bf16[256,2048]{1,0:T(8,128)(2,1)}, u32[]{:S(2)}, u32[]{:S(2)}) collective-permute-start(bf16[256,2048]{1,0:T(8,128)(2,1)S(1)} %fusion.19), channel_id=1, source_target_pairs={{0,1},{1,0},{2,3},{3,2},{4,5},{5,4},{6,7},{7,6},{8,9},{9,8},{10,11... | collective-permute-start | bytes 3145736 | tf_op jit(solution)/shard_map/ppermute | solution.py:462
  319.4 1.5 copy-start.6
  329.7 1.0 copy-start.13
Sparse Core Ops, SparseCore 0:
  10.0 266.8 all-gather.1

commit v3 on v2

--- a/solution.py
+++ b/solution.py
@@ -21,6 +21,7 @@
 
 MESH = pl.DeviceIdType.MESH
 KEY_TILE = 512
+HIDDEN_TILE = 700
 
 
 def greet_all(n, me):
@@ -350,6 +351,81 @@
     )
 
 
+def expert_kernel(tiles, x_ref, picked_ref, mix_ref, w_ref, gw_ref, uw_ref, ds_ref, out_ref, rank_ref, acc):
+    tile = pl.program_id(0)
+    x = x_ref[...]
+    gate = dot_t(w_ref[0], x)
+    up = dot_t(w_ref[1], x)
+    mixed = 0.0
+    ranks = []
+    for slot in range(2):
+        gate_one = gate + dot_t(gw_ref[...], picked_ref[slot])
+        up_one = up + dot_t(uw_ref[...], picked_ref[2 + slot])
+        hidden = jax.nn.silu(gate_one) * up_one
+        mixed = mixed + mix_ref[slot : slot + 1, :] * hidden
+        ranks.append(over_rows(hidden.astype(jnp.bfloat16), ds_ref[...]))
+    down = over_rows(mixed.astype(jnp.bfloat16), w_ref[2])
+
+    @pl.when(tile == 0)
+    def _():
+        acc[...] = down
+        for slot in range(2):
+            rank_ref[slot] = ranks[slot]
+
+    @pl.when(tile > 0)
+    def _():
+        acc[...] += down
+        for slot in range(2):
+            rank_ref[slot] += ranks[slot]
+
+    @pl.when(tile == tiles - 1)
+    def _():
+        out_ref[...] = acc[...].astype(out_ref.dtype)
+
+
+def over_rows(one, other):
+    return lax.dot_general(
+        one, other, (((0,), (0,)), ((), ())), preferred_element_type=jnp.float32
+    )
+
+
+def expert_layers(x, picked, mix, weights, gate_widen, up_widen, down_shrink):
+    rows, width = x.shape
+    units, columns = down_shrink.shape
+    size = max(
+        [t for t in range(16, min(units, HIDDEN_TILE) + 1, 16) if units % t == 0], default=units
+    )
+    return pl.pallas_call(
+        functools.partial(expert_kernel, units // size),
+        out_shape=(
+            jax.ShapeDtypeStruct((rows, width), jnp.bfloat16),
+            jax.ShapeDtypeStruct((2, rows, columns), jnp.float32),
+        ),
+        grid=(units // size,),
+        in_specs=[
+            pl.BlockSpec((rows, width), lambda i: (0, 0)),
+            pl.BlockSpec((4, rows, columns), lambda i: (0, 0, 0)),
+            pl.BlockSpec((2, rows), lambda i: (0, 0)),
+            pl.BlockSpec((3, size, width), lambda i: (0, i, 0)),
+            pl.BlockSpec((size, columns), lambda i: (i, 0)),
+            pl.BlockSpec((size, columns), lambda i: (i, 0)),
+            pl.BlockSpec((size, columns), lambda i: (i, 0)),
+        ],
+        out_specs=(
+            pl.BlockSpec((rows, width), lambda i: (0, 0)),
+            pl.BlockSpec((2, rows, columns), lambda i: (0, 0, 0)),
+        ),
+        scratch_shapes=[pltpu.VMEM((rows, width), jnp.float32)],
+        compiler_params=pltpu.CompilerParams(vmem_limit_bytes=48 * 1024 * 1024),
+        cost_estimate=pl.CostEstimate(
+            flops=6 * rows * width * units,
+            bytes_accessed=6 * units * width,
+            transcendentals=4 * rows * units,
+        ),
+        name="expert_layers",
+    )(x, picked, mix, weights, gate_widen.T, up_widen.T, down_shrink)
+
+
 def feed_forward(normed, routing, weights, router, gate_shrink, up_shrink, gate_widen_maps, upward_widen_maps, down_shrink):
     rank_gate = jnp.dot(normed, gate_shrink, preferred_element_type=jnp.float32).astype(
         jnp.bfloat16
@@ -361,39 +437,22 @@
     second_logit = jnp.sum(jnp.where(routing[:, 1:2] == expert_ids[None, :], logits, 0.0), axis=1)
     weight_first = jax.nn.sigmoid(first_logit - second_logit)[:, None]
     weight_second = jax.nn.sigmoid(second_logit - first_logit)[:, None]
-    frozen_gate_output = dot_t(normed, weights[0])
-    frozen_up_output = dot_t(normed, weights[1])
     column_expert = jnp.arange(EXPERTS * RANK, dtype=jnp.int32) // RANK
-    hiddens = []
-    pickers = []
-    for slot_index in range(2):
-        picker = column_expert[None, :] == routing[:, slot_index : slot_index + 1]
-        pickers.append(picker)
-        selected_gate_widen = jnp.where(picker, rank_gate, jnp.zeros_like(rank_gate))
-        selected_upward_widen = jnp.where(picker, rank_up, jnp.zeros_like(rank_up))
-        gate_complete_output = frozen_gate_output + adapter_scale_factor * jnp.dot(
-            selected_gate_widen, gate_widen_maps, preferred_element_type=jnp.float32
-        )
-        upward_complete_output = frozen_up_output + adapter_scale_factor * jnp.dot(
-            selected_upward_widen, upward_widen_maps, preferred_element_type=jnp.float32
-        )
-        hiddens.append(jax.nn.silu(gate_complete_output) * upward_complete_output)
-    mixture = (weight_first * hiddens[0] + weight_second * hiddens[1]).astype(jnp.bfloat16)
-    shrunk_first = jnp.dot(
-        hiddens[0].astype(jnp.bfloat16), down_shrink, preferred_element_type=jnp.float32
-    )
-    shrunk_second = jnp.dot(
-        hiddens[1].astype(jnp.bfloat16), down_shrink, preferred_element_type=jnp.float32
-    )
-    rank_down = weight_first * jnp.where(pickers[0], shrunk_first, 0.0) + weight_second * jnp.where(
-        pickers[1], shrunk_second, 0.0
-    )
-    downward_adapter_term = jnp.dot(
-        mixture,
-        weights[2],
-        preferred_element_type=jnp.float32,
-    )
-    return downward_adapter_term.astype(jnp.bfloat16), rank_down.astype(jnp.bfloat16)
+    pickers = [column_expert[None, :] == routing[:, slot : slot + 1] for slot in range(2)]
+    picked = [
+        jnp.where(picker, adapter_scale_factor * ranks, jnp.zeros_like(ranks))
+        for ranks in (rank_gate, rank_up)
+        for picker in pickers
+    ]
+    mix_weights = jnp.stack((weight_first[:, 0], weight_second[:, 0]))
+    down_sum, shrunk = expert_layers(
+        normed, jnp.stack(picked), mix_weights, weights, gate_widen_maps, upward_widen_maps, down_shrink
+    )
+    rank_down = weight_first * jnp.where(pickers[0], shrunk[0], 0.0) + weight_second * jnp.where(
+        pickers[1], shrunk[1], 0.0
+    )
+    return down_sum, rank_down.astype(jnp.bfloat16)
+
 
 def on_device(
     queries,

time: 343 us -> 334 us (0.974)
  matrix products: 65.2 us -> 13.9 us
  Pallas kernels: 179 us -> 212 us
  waiting for transfers between devices: 66.6 us -> 71.8 us
    dot_general x17 -> x0, matrix products: 49.3 us -> none  [the longest x4 24.7 us: dot_t(): lax.dot_general(rows, other, (((1,), (1,)), ((), ())), preferred_element_...]
    pallas_call x0 -> x2, Pallas kernels: none -> 36 us  [expert_layers(): pl.pallas_call(functools.partial(expert_kernel, units // size), out_shape...]
    pallas_call x1, Pallas kernels: 37.9 us -> 30.9 us  [attend(): pl.pallas_call(functools.partial(attend_kernel, tokens, part, docs), out_...]
    ppermute x2, waiting for transfers between devices: 0.01 us -> 5.22 us  [on_device(): come = [lax.ppermute(part_sum, 'tp', swap) for part_sum in away]]
    pallas_call x1, Pallas kernels: 61 us -> 65.4 us  [regather(): pl.pallas_call(functools.partial(gather_kernel, n, tn, group, heads, tn =...]
    dot_general x1, matrix products: 5.29 us -> 1.61 us  [on_device(): jnp.dot(rank_rows.astype(jnp.bfloat16), down_expand, preferred_element_ty...]
  transfers between devices with their start and end apart: 5 -> 5, of which waited for: 2 -> 3; matrix products, arithmetic and copies ran while one was open for 11% -> 5% of each run, Pallas kernels for 52% -> 58%
where the time goes in v3:
time: 334 us
  Pallas kernels  212 us (63%)
  waiting for transfers between devices  71.8 us (21%)
  matrix products  13.9 us (4%)
  between operations  13.7 us (4%)
  local copies, waits for them, and re-layouts  9.77 us (3%)
  starting transfers between devices  6.34 us (2%)
  other arithmetic  6.24 us (2%)
    pallas_call x1, Pallas kernels, spread(): pl.pallas_call(functools.partial(spread_kernel, n, group), out_shape=(jax...  79.6 us
    pallas_call x1, Pallas kernels, regather(): pl.pallas_call(functools.partial(gather_kernel, n, tn, group, heads, tn =...  65.4 us
    all_gather x1, waiting for transfers between devices, on_device(): lax.all_gather(jnp.stack((gate_weight.T, up_weight.T, down_weight)), 'seq...  42.5 us
    pallas_call x2, Pallas kernels, expert_layers(): pl.pallas_call(functools.partial(expert_kernel, units // size), out_shape...  36 us
    pallas_call x1, Pallas kernels, attend(): pl.pallas_call(functools.partial(attend_kernel, tokens, part, docs), out_...  30.9 us
    ppermute x1, waiting for transfers between devices, on_device(): normed_away = lax.ppermute(normed_own, 'tp', swap)  24 us
    unnamed x40, local copies, waits for them, and re-layouts  9.69 us
  transfers between devices with their start and end apart: 5, of which 3 were waited for; matrix products, arithmetic and copies ran while one was open for 5% of the time, Pallas kernels for 58%

profile of v3, /device:TPU:0, one launch (start us, length us, event | category | flops | bytes accessed | tf_op | source)
XLA Modules:
  0.0 333.6 jit_solution(5928926801537332396)
XLA Ops:
  6.5 0.0 all-gather.2.cloned.1.call-start
  6.5 3.2 pad_maximum_fusion
  9.7 0.0 all-gather.2.cloned.1.call-update
  9.8 3.0 collective-permute-start
  12.8 0.2 reduce-window.9
  13.0 1.5 pad_maximum_fusion.1.kv_ref
  14.5 79.6 %spread_heads.1 = (bf16[4096,128]{1,0:T(8,128)(2,1)}, bf16[2,8192,128]{2,1,0:T(8,128)(2,1)}) custom-call(bf16[512,1024]{1,0:T(8,128)(2,1)} %q_ref.1, bf16[2,512,1024]{2,1,0:T(8,128)(2,1)} %pad_maximum_fusion.1.kv_ref), custom_call_target="tpu_custom_call" | custom-call | bytes 200000000 | tf_op jit(solution)/shard_map/spread_heads/pallas_call | solution.py:145
  94.1 0.1 pad_add_fusion.scalars
  94.2 3.0 copy-done.6
  97.1 1.2 copy-done.7
  98.4 30.9 %attend_docs.1.x_ref = bf16[4096,128]{1,0:T(8,128)(2,1)S(1)} custom-call(s32[5]{0:T(128)S(1)} %pad_add_fusion.scalars, bf16[4096,128]{1,0:T(8,128)(2,1)S(1)} %copy-done.7, bf16[2,8192,128]{2,1,0:T(8,128)(2,1)S(1)} %copy-done.6, bf16[2,8192,128]{2,1,0:T(8,128)(2,1)S(1)} %copy-done.6), custom_call_target="tpu_custom_call" | custom-call | flops 20000000000 | bytes 8000000 | tf_op jit(solution)/shard_map/attend_docs/pallas_call | solution.py:327
  129.3 0.0 copy-start.5
  129.4 1.0 copy-done.5
  130.3 65.4 %regather_heads.1 = bf16[256,2048]{1,0:T(8,128)(2,1)} custom-call(bf16[4096,128]{1,0:T(8,128)(2,1)} %copy-done.5), custom_call_target="tpu_custom_call" | custom-call | bytes 60000000 | tf_op jit(solution)/shard_map/regather_heads/pallas_call | solution.py:267
  195.8 0.0 copy-start.18
  195.8 3.7 %fusion.6 = f32[256,2048]{1,0:T(8,128)S(1)} fusion(bf16[1024,2048]{1,0:T(8,128)(2,1)} %param.22, bf16[256,2048]{1,0:T(8,128)(2,1)} %regather_heads.1), kind=kOutput, calls=%fused_computation.17 | convolution fusion | flops 1073741824 | bytes 6815744 | tf_op jit(solution)/shard_map/dot_general | solution.py:498
  199.5 0.0 copy-start.16
  199.5 0.0 collective-permute-done
  199.6 3.8 %multiply_reduce_fusion = (f32[256]{0:T(256)S(1)}, f32[256,2048]{1,0:T(8,128)S(1)}) fusion(f32[256,2048]{1,0:T(8,128)S(1)} %fusion.6, bf16[1024,2048]{1,0:T(8,128)(2,1)} %collective-permute-done, bf16[256,2048]{1,0:T(8,128)(2,1)S(1)} %copy-done.12, bf16[256,2048]{1,0:T(8,128)(2,1)S(1)} %copy-done.18), kind=kOutput, calls=%fused_computation.7 | convolution fusion | flops 1076363008 | bytes 9962496 | tf_op jit(solution)/shard_map/dot_general | solution.py:500
  203.4 0.0 copy-start.17
  203.4 0.0 copy-start.15
  203.4 1.3 copy-done.8
  204.7 0.2 multiply_convert_fusion.x_ref
  205.0 1.2 collective-permute-start.1
  206.2 0.0 copy-done.17
  206.2 0.1 constant_dynamic-slice_fusion.1
  206.3 24.0 %collective-permute-done.1.x_ref = bf16[256,2048]{1,0:T(8,128)(2,1)S(1)} collective-permute-done((bf16[256,2048]{1,0:T(8,128)(2,1)S(1)}, bf16[256,2048]{1,0:T(8,128)(2,1)S(1)}, u32[]{:S(2)}, u32[]{:S(2)}) %collective-permute-start.1) | collective-permute-done | bytes 1048608 | tf_op jit(solution)/shard_map/ppermute | solution.py:517
  230.3 0.4 select_reduce_fusion.3
  230.7 0.0 copy-start.1
  230.8 1.5 fusion.1
  232.3 1.5 fusion.18
  233.8 0.7 pad_maximum_fusion.2.picked_ref
  234.5 42.5 %all-gather.2.cloned.1.call-done.w_ref = bf16[3,2752,2048]{2,1,0:T(8,128)(2,1)} async-done(((bf16[3,2752,128]{2,1,0:T(8,128)(2,1)}), bf16[3,2752,2048]{2,1,0:T(8,128)(2,1)}) %all-gather.2.cloned.1.call-update) | async-done | bytes 33816592 | tf_op jit(solution)/shard_map/all_gather | solution.py:485
  277.1 1.1 copy-done.2
  278.2 1.1 copy-done.3
  279.3 0.9 copy-done.4
  280.2 17.9 %expert_layers.2 = (bf16[256,2048]{1,0:T(8,128)(2,1)S(1)}, f32[2,256,128]{2,1,0:T(8,128)S(1)}) custom-call(bf16[256,2048]{1,0:T(8,128)(2,1)S(1)} %collective-permute-done.1.x_ref, bf16[4,256,128]{2,1,0:T(8,128)(2,1)S(1)} %copy-done.4, f32[2,256]{1,0:T(2,128)S(1)} %pad_maximum_fusion.4.mix_ref, bf16[3,2752,2048]{2,1,0:T(8,128)(2,1)} %all-gather.2.cloned.1.call-done.w_ref, ...), custom_call_target="tpu_custom_call" | custom-call | flops 8657043456 | bytes 33816576 | tf_op jit(solution)/shard_map/expert_layers/pallas_call | solution.py:398
  298.1 0.0 copy-start.11
  298.2 0.2 fusion.10
  298.4 1.3 collective-permute-start.3
  299.7 0.8 collective-permute-start.2
  300.5 0.4 fusion.3
  300.9 0.4 select_reduce_fusion.1
  301.3 0.4 fusion.22
  301.8 18.1 %expert_layers.3 = (bf16[256,2048]{1,0:T(8,128)(2,1)S(1)}, f32[2,256,128]{2,1,0:T(8,128)S(1)}) custom-call(bf16[256,2048]{1,0:T(8,128)(2,1)S(1)} %multiply_convert_fusion.x_ref, bf16[4,256,128]{2,1,0:T(8,128)(2,1)S(1)} %pad_maximum_fusion.3.picked_ref, f32[2,256]{1,0:T(2,128)S(1)} %pad_maximum_fusion.5.mix_ref, ...), custom_call_target="tpu_custom_call" | custom-call | flops 8657043456 | bytes 33816576 | tf_op jit(solution)/shard_map/expert_layers/pallas_call | solution.py:398
  319.9 0.0 collective-permute-done.3
  320.0 5.2 %collective-permute-done.2 = bf16[256,2048]{1,0:T(8,128)(2,1)S(1)} collective-permute-done((bf16[256,2048]{1,0:T(8,128)(2,1)S(1)}, bf16[256,2048]{1,0:T(8,128)(2,1)S(1)}, u32[]{:S(2)}, u32[]{:S(2)}) %collective-permute-start.2) | collective-permute-done | bytes 1048608 | tf_op jit(solution)/shard_map/ppermute | solution.py:521
  325.2 1.6 add_convert_fusion
  (32 shorter events, 0.1 us)
Async XLA Ops:
  6.5 318.6 %copy-start = (bf16[128,2048]{1,0:T(8,128)(2,1)S(1)}, bf16[128,2048]{1,0:T(8,128)(2,1)}, u32[]{:S(2)}) copy-start(bf16[128,2048]{1,0:T(8,128)(2,1)} %param.33) | copy-start | bytes 1572868
  6.5 270.5 %all-gather.2.cloned.1.call-start = ((), (), s32[]{:S(2)}) async-start(), calls=%async_computation | async-start | bytes 35930112 | tf_op jit(solution)/shard_map/all_gather | solution.py:485
  9.7 3.1 copy-start.19
  9.7 3.2 copy-start.13
  9.7 3.2 copy-start.14
  9.8 189.8 %collective-permute-start = (bf16[1024,2048]{1,0:T(8,128)(2,1)}, bf16[1024,2048]{1,0:T(8,128)(2,1)}, u32[]{:S(2)}, u32[]{:S(2)}) collective-permute-start(bf16[1024,2048]{1,0:T(8,128)(2,1)} %param.22), channel_id=1, source_target_pairs={{0,1},{1,0},{2,3},{3,2},{4,5},{5,4},{6,7},{7,6},{8,9},{9,8},{10,11... | collective-permute-start | bytes 12582920 | tf_op jit(solution)/shard_map/ppermute | solution.py:497
  94.2 3.0 copy-start.6
  97.1 1.2 copy-start.7
  129.3 1.0 copy-start.5
  195.8 3.8 %copy-start.12 = (bf16[256,2048]{1,0:T(8,128)(2,1)S(1)}, bf16[256,2048]{1,0:T(8,128)(2,1)}, u32[]{:S(2)}) copy-start(bf16[256,2048]{1,0:T(8,128)(2,1)} %regather_heads.1) | copy-start | bytes 3145732
  195.8 3.8 %copy-start.18 = (bf16[256,2048]{1,0:T(8,128)(2,1)S(1)}, bf16[256,2048]{1,0:T(8,128)(2,1)}, u32[]{:S(2)}) copy-start(bf16[256,2048]{1,0:T(8,128)(2,1)} %param.21) | copy-start | bytes 3145732
  199.5 5.2 %copy-start.16 = (f32[2048]{0:T(1024)S(1)}, f32[2048]{0:T(1024)}, u32[]{:S(2)}) copy-start(f32[2048]{0:T(1024)} %param.23) | copy-start | bytes 24580
  203.4 1.3 copy-start.8
  203.4 2.8 copy-start.17
  203.4 26.9 %copy-start.15 = (bf16[2048,8]{0,1:T(8,128)(2,1)S(1)}, bf16[2048,8]{0,1:T(8,128)(2,1)}, u32[]{:S(2)}) copy-start(bf16[2048,8]{0,1:T(8,128)(2,1)} %param.24) | copy-start | bytes 98308
  205.0 25.3 %collective-permute-start.1 = (bf16[256,2048]{1,0:T(8,128)(2,1)S(1)}, bf16[256,2048]{1,0:T(8,128)(2,1)S(1)}, u32[]{:S(2)}, u32[]{:S(2)}) collective-permute-start(bf16[256,2048]{1,0:T(8,128)(2,1)S(1)} %multiply_convert_fusion.x_ref), channel_id=1, source_target_pairs={{0,1},{1,0},{2,3},{3,2},{4,5},{5,4},{6,7},{7,6},{8,9},{9,8},{10,11... | collective-permute-start | bytes 3145736 | tf_op jit(solution)/shard_map/ppermute | solution.py:517
  230.7 46.3 %copy-start.1 = (bf16[128,2752]{0,1:T(8,128)(2,1)S(1)}, bf16[128,2752]{0,1:T(8,128)(2,1)}, u32[]{:S(2)}) copy-start(bf16[128,2752]{0,1:T(8,128)(2,1)} %param.30) | copy-start | bytes 2113540
  277.1 1.1 copy-start.2
  278.2 1.1 copy-start.3
  279.3 0.9 copy-start.4
  280.2 20.3 %copy-start.10 = (bf16[2048,128]{1,0:T(8,128)(2,1)S(1)}, bf16[2048,128]{1,0:T(8,128)(2,1)}, u32[]{:S(2)}) copy-start(bf16[2048,128]{1,0:T(8,128)(2,1)} %param.28) | copy-start | bytes 1572868
  298.1 3.2 copy-start.11
  298.4 21.6 %collective-permute-start.3 = (bf16[256,128]{1,0:T(8,128)(2,1)S(1)}, bf16[256,128]{1,0:T(8,128)(2,1)S(1)}, u32[]{:S(2)}, u32[]{:S(2)}) collective-permute-start(bf16[256,128]{1,0:T(8,128)(2,1)S(1)} %fusion.10), channel_id=1, source_target_pairs={{0,1},{1,0},{2,3},{3,2},{4,5},{5,4},{6,7},{7,6},{8,9},{9,8},{10,11... | collective-permute-start | bytes 196616 | tf_op jit(solution)/shard_map/ppermute | solution.py:521
  299.7 25.5 %collective-permute-start.2 = (bf16[256,2048]{1,0:T(8,128)(2,1)S(1)}, bf16[256,2048]{1,0:T(8,128)(2,1)S(1)}, u32[]{:S(2)}, u32[]{:S(2)}) collective-permute-start(bf16[256,2048]{1,0:T(8,128)(2,1)S(1)} %get-tuple-element.14), channel_id=1, source_target_pairs={{0,1},{1,0},{2,3},{3,2},{4,5},{5,4},{6,7},{7,6},{8,9},{9,8},{10,11... | collective-permute-start | bytes 3145736 | tf_op jit(solution)/shard_map/ppermute | solution.py:521
  301.8 23.4 %copy-start.9 = (f32[256,2048]{1,0:T(8,128)S(1)}, f32[256,2048]{1,0:T(8,128)}, u32[]{:S(2)}) copy-start(f32[256,2048]{1,0:T(8,128)} %copy-done.8) | copy-start | bytes 6291460
Sparse Core Ops, SparseCore 0:
  9.9 267.1 all-gather.1

commit v4 on v3

--- a/solution.py
+++ b/solution.py
@@ -416,7 +416,7 @@
             pl.BlockSpec((2, rows, columns), lambda i: (0, 0, 0)),
         ),
         scratch_shapes=[pltpu.VMEM((rows, width), jnp.float32)],
-        compiler_params=pltpu.CompilerParams(vmem_limit_bytes=48 * 1024 * 1024),
+        compiler_params=pltpu.CompilerParams(vmem_limit_bytes=63 * 1024 * 1024),
         cost_estimate=pl.CostEstimate(
             flops=6 * rows * width * units,
             bytes_accessed=6 * units * width,
@@ -426,7 +426,7 @@
     )(x, picked, mix, weights, gate_widen.T, up_widen.T, down_shrink)
 
 
-def feed_forward(normed, routing, weights, router, gate_shrink, up_shrink, gate_widen_maps, upward_widen_maps, down_shrink):
+def feed_forward(normed, routing, weights, router, gate_shrink, up_shrink, gate_widen_maps, upward_widen_maps, down_shrink, after=()):
     rank_gate = jnp.dot(normed, gate_shrink, preferred_element_type=jnp.float32).astype(
         jnp.bfloat16
     )
@@ -445,6 +445,7 @@
         for picker in pickers
     ]
     mix_weights = jnp.stack((weight_first[:, 0], weight_second[:, 0]))
+    normed, _ = lax.optimization_barrier((normed, after))
     down_sum, shrunk = expert_layers(
         normed, jnp.stack(picked), mix_weights, weights, gate_widen_maps, upward_widen_maps, down_shrink
     )
@@ -519,8 +520,7 @@
         routing_away = lax.dynamic_slice_in_dim(routing, (1 - me) * half, half, 0)
         away = feed_forward(normed_away, routing_away, weights, *shared)
         come = [lax.ppermute(part_sum, "tp", swap) for part_sum in away]
-        normed_own, _ = lax.optimization_barrier((normed_own, away))
-        here = feed_forward(normed_own, routing_own, weights, *shared)
+        here = feed_forward(normed_own, routing_own, weights, *shared, after=away)
         downward_token_rows, rank_rows = [
             one.astype(jnp.float32) + two.astype(jnp.float32) for one, two in zip(here, come)
         ]

time: 334 us -> 334 us (level)
  Pallas kernels: 212 us -> 217 us
  waiting for transfers between devices: 71.8 us -> 66.9 us
    pallas_call x1, Pallas kernels: 30.9 us -> 37.9 us  [attend(): pl.pallas_call(functools.partial(attend_kernel, tokens, part, docs), out_...]
    pallas_call x1, Pallas kernels: 65.4 us -> 61 us  [regather(): pl.pallas_call(functools.partial(gather_kernel, n, tn, group, heads, tn =...]
    unnamed x40 -> x34, local copies, waits for them, and re-layouts: 9.69 us -> 6.63 us
  transfers between devices with their start and end apart: 5 -> 5, of which waited for: 3 -> 3; matrix products, arithmetic and copies ran while one was open for 5% -> 5% of each run, Pallas kernels for 58% -> 59%
where the time goes in v4:
time: 334 us
  Pallas kernels  217 us (65%)
  waiting for transfers between devices  66.9 us (20%)
  matrix products  14.4 us (4%)
  between operations  13.6 us (4%)
  other arithmetic  8.37 us (3%)
  local copies, waits for them, and re-layouts  6.7 us (2%)
  starting transfers between devices  6.48 us (2%)
    pallas_call x1, Pallas kernels, spread(): pl.pallas_call(functools.partial(spread_kernel, n, group), out_shape=(jax...  79.6 us
    pallas_call x1, Pallas kernels, regather(): pl.pallas_call(functools.partial(gather_kernel, n, tn, group, heads, tn =...  61 us
    all_gather x1, waiting for transfers between devices, on_device(): lax.all_gather(jnp.stack((gate_weight.T, up_weight.T, down_weight)), 'seq...  41.2 us
    pallas_call x2, Pallas kernels, expert_layers(): pl.pallas_call(functools.partial(expert_kernel, units // size), out_shape...  38.9 us
    pallas_call x1, Pallas kernels, attend(): pl.pallas_call(functools.partial(attend_kernel, tokens, part, docs), out_...  37.9 us
    ppermute x1, waiting for transfers between devices, on_device(): normed_away = lax.ppermute(normed_own, 'tp', swap)  22.1 us
  transfers between devices with their start and end apart: 5, of which 3 were waited for; matrix products, arithmetic and copies ran while one was open for 5% of the time, Pallas kernels for 59%

profile of v4, /device:TPU:0, one launch (start us, length us, event | category | flops | bytes accessed | tf_op | source)
XLA Modules:
  0.0 333.9 jit_solution(8979741160838121180)
XLA Ops:
  6.5 0.0 copy-start
  6.5 3.2 pad_maximum_fusion
  9.7 0.0 all-gather.2.cloned.1.call-update
  9.7 3.0 collective-permute-start
  12.8 0.2 reduce-window.9
  13.0 0.0 copy-done.11
  13.0 1.5 pad_maximum_fusion.1.kv_ref
  14.5 79.6 %spread_heads.1 = (bf16[4096,128]{1,0:T(8,128)(2,1)}, bf16[2,8192,128]{2,1,0:T(8,128)(2,1)}) custom-call(bf16[512,1024]{1,0:T(8,128)(2,1)} %q_ref.1, bf16[2,512,1024]{2,1,0:T(8,128)(2,1)} %pad_maximum_fusion.1.kv_ref), custom_call_target="tpu_custom_call" | custom-call | bytes 200000000 | tf_op jit(solution)/shard_map/spread_heads/pallas_call | solution.py:145
  94.1 0.1 pad_add_fusion.scalars
  94.2 3.0 copy-done.2
  97.1 1.2 copy-done.3
  98.4 37.9 %attend_docs.1.x_ref = bf16[4096,128]{1,0:T(8,128)(2,1)S(1)} custom-call(s32[5]{0:T(128)S(1)} %pad_add_fusion.scalars, bf16[4096,128]{1,0:T(8,128)(2,1)S(1)} %copy-done.3, bf16[2,8192,128]{2,1,0:T(8,128)(2,1)S(1)} %copy-done.2, bf16[2,8192,128]{2,1,0:T(8,128)(2,1)S(1)} %copy-done.2), custom_call_target="tpu_custom_call" | custom-call | flops 20000000000 | bytes 8000000 | tf_op jit(solution)/shard_map/attend_docs/pallas_call | solution.py:327
  136.3 0.0 copy-start.1
  136.3 1.0 copy-done.1
  137.3 61.0 %regather_heads.1 = bf16[256,2048]{1,0:T(8,128)(2,1)} custom-call(bf16[4096,128]{1,0:T(8,128)(2,1)} %copy-done.1), custom_call_target="tpu_custom_call" | custom-call | bytes 60000000 | tf_op jit(solution)/shard_map/regather_heads/pallas_call | solution.py:267
  198.3 0.0 copy-start.9
  198.3 0.0 copy-start.15
  198.3 4.3 %fusion.6 = f32[256,2048]{1,0:T(8,128)S(1)} fusion(bf16[1024,2048]{1,0:T(8,128)(2,1)} %param.22, bf16[256,2048]{1,0:T(8,128)(2,1)} %regather_heads.1), kind=kOutput, calls=%fused_computation.17 | convolution fusion | flops 1073741824 | bytes 6815744 | tf_op jit(solution)/shard_map/dot_general | solution.py:499
  202.6 0.0 copy-start.13
  202.7 0.0 collective-permute-done
  202.7 3.7 %multiply_reduce_fusion = (f32[256]{0:T(256)S(1)}, f32[256,2048]{1,0:T(8,128)S(1)}) fusion(f32[256,2048]{1,0:T(8,128)S(1)} %fusion.6, bf16[1024,2048]{1,0:T(8,128)(2,1)} %collective-permute-done, bf16[256,2048]{1,0:T(8,128)(2,1)S(1)} %copy-done.9, bf16[256,2048]{1,0:T(8,128)(2,1)S(1)} %copy-done.15), kind=kOutput, calls=%fused_computation.7 | convolution fusion | flops 1076363008 | bytes 9962496 | tf_op jit(solution)/shard_map/dot_general | solution.py:501
  206.4 0.0 copy-start.14
  206.4 0.0 copy-start.12
  206.4 1.3 copy-done.6
  207.7 0.0 copy-done.13
  207.7 0.2 multiply_convert_fusion.x_ref
  208.0 1.4 collective-permute-start.1
  209.3 0.1 constant_dynamic-slice_fusion.1
  209.4 0.4 select_reduce_fusion.1
  209.8 0.4 fusion.4
  210.3 0.1 copy-done.8
  210.4 0.4 fusion.3
  210.8 22.1 %collective-permute-done.1.x_ref = bf16[256,2048]{1,0:T(8,128)(2,1)S(1)} collective-permute-done((bf16[256,2048]{1,0:T(8,128)(2,1)S(1)}, bf16[256,2048]{1,0:T(8,128)(2,1)S(1)}, u32[]{:S(2)}, u32[]{:S(2)}) %collective-permute-start.1) | collective-permute-done | bytes 1048608 | tf_op jit(solution)/shard_map/ppermute | solution.py:518
  232.9 0.4 select_reduce_fusion.3
  233.4 0.5 pad_maximum_fusion.4.mix_ref
  233.9 0.4 fusion.2
  234.3 0.4 fusion.22
  234.8 0.9 pad_maximum_fusion.2
  235.6 41.2 %all-gather.2.cloned.1.call-done.w_ref = bf16[3,2752,2048]{2,1,0:T(8,128)(2,1)} async-done(((bf16[3,2752,128]{2,1,0:T(8,128)(2,1)}), bf16[3,2752,2048]{2,1,0:T(8,128)(2,1)}) %all-gather.2.cloned.1.call-update) | async-done | bytes 33816592 | tf_op jit(solution)/shard_map/all_gather | solution.py:486
  276.8 19.5 %expert_layers.2 = (bf16[256,2048]{1,0:T(8,128)(2,1)}, f32[2,256,128]{2,1,0:T(8,128)}) custom-call(bf16[256,2048]{1,0:T(8,128)(2,1)} %copy-done.5, bf16[4,256,128]{2,1,0:T(8,128)(2,1)} %get-tuple-element.49.picked_ref, f32[2,256]{1,0:T(2,128)} %pad_maximum_fusion.4.mix_ref, bf16[3,2752,2048]{2,1,0:T(8,128)(2,1)} %all-gather.2.cloned.1.call-done.w_ref, ...), custom_call_target="tpu_custom_call" | custom-call | flops 8657043456 | bytes 33816576 | tf_op jit(solution)/shard_map/expert_layers/pallas_call | solution.py:398
  296.2 1.2 collective-permute-start.2
  297.4 0.6 pad_maximum_fusion.5.mix_ref
  298.0 1.2 fusion.10
  299.2 0.9 collective-permute-start.3
  300.1 19.5 %expert_layers.3 = (bf16[256,2048]{1,0:T(8,128)(2,1)}, f32[2,256,128]{2,1,0:T(8,128)}) custom-call(bf16[256,2048]{1,0:T(8,128)(2,1)} %copy-done.4, bf16[4,256,128]{2,1,0:T(8,128)(2,1)} %get-tuple-element.50.picked_ref, f32[2,256]{1,0:T(2,128)} %pad_maximum_fusion.5.mix_ref, bf16[3,2752,2048]{2,1,0:T(8,128)(2,1)} %all-gather.2.cloned.1.call-done.w_ref, ...), custom_call_target="tpu_custom_call" | custom-call | flops 8657043456 | bytes 33816576 | tf_op jit(solution)/shard_map/expert_layers/pallas_call | solution.py:398
  319.6 3.6 %collective-permute-done.3 = bf16[256,128]{1,0:T(8,128)(2,1)S(1)} collective-permute-done((bf16[256,128]{1,0:T(8,128)(2,1)S(1)}, bf16[256,128]{1,0:T(8,128)(2,1)S(1)}, u32[]{:S(2)}, u32[]{:S(2)}) %collective-permute-start.3) | collective-permute-done | bytes 65568 | tf_op jit(solution)/shard_map/ppermute | solution.py:522
  323.2 0.0 collective-permute-done.2
  323.2 3.9 %add_convert_fusion = bf16[256,2048]{1,0:T(8,128)(2,1)} fusion(f32[256,2048]{1,0:T(8,128)} %copy-done.6, bf16[256,2048]{1,0:T(8,128)(2,1)} %collective-permute-done.2, bf16[256,2048]{1,0:T(8,128)(2,1)} %get-tuple-element.17, bf16[128,2048]{1,0:T(8,128)(2,1)S(1)} %copy-done, bf16[256,128]{1,0:T(8,128)(2,1)S(1)} %collective-permute-done.3, ...), kind=kOutput, calls=%fused_computation.5 | convolution fusion | flops 138280960 | bytes 6099456 | tf_op jit(solution)/shard_map/dot_general | solution.py:533
  (25 shorter events, 0.1 us)
Async XLA Ops:
  6.5 316.7 %copy-start = (bf16[128,2048]{1,0:T(8,128)(2,1)S(1)}, bf16[128,2048]{1,0:T(8,128)(2,1)}, u32[]{:S(2)}) copy-start(bf16[128,2048]{1,0:T(8,128)(2,1)} %param.33) | copy-start | bytes 1572868
  6.5 270.3 %all-gather.2.cloned.1.call-start = ((), (), s32[]{:S(2)}) async-start(), calls=%async_computation | async-start | bytes 35930112 | tf_op jit(solution)/shard_map/all_gather | solution.py:486
  9.7 3.1 copy-start.16
  9.7 3.2 copy-start.10
  9.7 3.2 copy-start.11
  9.7 192.9 %collective-permute-start = (bf16[1024,2048]{1,0:T(8,128)(2,1)}, bf16[1024,2048]{1,0:T(8,128)(2,1)}, u32[]{:S(2)}, u32[]{:S(2)}) collective-permute-start(bf16[1024,2048]{1,0:T(8,128)(2,1)} %param.22), channel_id=1, source_target_pairs={{0,1},{1,0},{2,3},{3,2},{4,5},{5,4},{6,7},{7,6},{8,9},{9,8},{10,11... | collective-permute-start | bytes 12582920 | tf_op jit(solution)/shard_map/ppermute | solution.py:498
  94.2 3.0 copy-start.2
  97.1 1.2 copy-start.3
  136.3 1.0 copy-start.1
  198.3 4.4 %copy-start.9 = (bf16[256,2048]{1,0:T(8,128)(2,1)S(1)}, bf16[256,2048]{1,0:T(8,128)(2,1)}, u32[]{:S(2)}) copy-start(bf16[256,2048]{1,0:T(8,128)(2,1)} %regather_heads.1) | copy-start | bytes 3145732
  198.3 4.4 %copy-start.15 = (bf16[256,2048]{1,0:T(8,128)(2,1)S(1)}, bf16[256,2048]{1,0:T(8,128)(2,1)}, u32[]{:S(2)}) copy-start(bf16[256,2048]{1,0:T(8,128)(2,1)} %param.21) | copy-start | bytes 3145732
  202.6 5.1 %copy-start.13 = (f32[2048]{0:T(1024)S(1)}, f32[2048]{0:T(1024)}, u32[]{:S(2)}) copy-start(f32[2048]{0:T(1024)} %param.23) | copy-start | bytes 24580
  206.4 1.3 copy-start.6
  206.4 2.9 copy-start.14
  206.4 3.0 copy-start.12
  207.7 2.1 copy-start.7
  208.0 2.8 copy-start.4
  208.0 25.0 %collective-permute-start.1 = (bf16[256,2048]{1,0:T(8,128)(2,1)S(1)}, bf16[256,2048]{1,0:T(8,128)(2,1)S(1)}, u32[]{:S(2)}, u32[]{:S(2)}) collective-permute-start(bf16[256,2048]{1,0:T(8,128)(2,1)S(1)} %multiply_convert_fusion.x_ref), channel_id=1, source_target_pairs={{0,1},{1,0},{2,3},{3,2},{4,5},{5,4},{6,7},{7,6},{8,9},{9,8},{10,11... | collective-permute-start | bytes 3145736 | tf_op jit(solution)/shard_map/ppermute | solution.py:518
  209.3 1.0 copy-start.8
  232.9 1.8 copy-start.5
  296.2 26.9 %collective-permute-start.2 = (bf16[256,2048]{1,0:T(8,128)(2,1)}, bf16[256,2048]{1,0:T(8,128)(2,1)}, u32[]{:S(2)}, u32[]{:S(2)}) collective-permute-start(bf16[256,2048]{1,0:T(8,128)(2,1)} %get-tuple-element.14), channel_id=1, source_target_pairs={{0,1},{1,0},{2,3},{3,2},{4,5},{5,4},{6,7},{7,6},{8,9},{9,8},{10,11... | collective-permute-start | bytes 3145736 | tf_op jit(solution)/shard_map/ppermute | solution.py:522
  299.2 24.0 %collective-permute-start.3 = (bf16[256,128]{1,0:T(8,128)(2,1)S(1)}, bf16[256,128]{1,0:T(8,128)(2,1)S(1)}, u32[]{:S(2)}, u32[]{:S(2)}) collective-permute-start(bf16[256,128]{1,0:T(8,128)(2,1)S(1)} %fusion.10), channel_id=1, source_target_pairs={{0,1},{1,0},{2,3},{3,2},{4,5},{5,4},{6,7},{7,6},{8,9},{9,8},{10,11... | collective-permute-start | bytes 196616 | tf_op jit(solution)/shard_map/ppermute | solution.py:522
Sparse Core Ops, SparseCore 0:
  9.9 266.8 all-gather.1
